TPU v7x, 32 devices: a whole 2x2x4 slice. The times are simulated.
32 devices in a mesh: row: 16 (over z, x, core), col: 2 (over y).
Axes of the slice: x: 2, y: 2, z: 4, core: 2. Of those that a mesh axis runs over, the one named last changes fastest.
Arguments:
- features: bfloat16 [16384, 256], P(('row', 'col')), may hold values from -6 to 6
- grad_out: bfloat16 [16384, 256], P(('row', 'col')), may hold values from -6 to 6
- weight: bfloat16 [256, 256], replicated, may hold values from -0.375 to 0.375
- tiles: bfloat16 [6144, 128, 128], P(('row', 'col')), may hold values from -0.125 to 0.125
- tile_row: int32 [6144], P(('row', 'col')), may hold values from 0 to 7
- tile_col: int32 [6144], P(('row', 'col')), may hold values from 0 to 63
- tile_count: int32 [32], P(('row', 'col')), may hold values from 24 to 192, as said below
Outputs:
- grad_features: bfloat16 [16384, 256], P(('row', 'col'))
- grad_weight: float32 [256, 256], replicated
Inputs may be any that keep to these rules, and one draw needn't show every extreme that they name: `tile_count`: exactly 192 on some device in every draw; slots of a device from its count on are not part of the adjacency.
All inputs are finite; a program needn't handle non-finite values.
Results may differ from a plain program's by a relative error of at most 0.02.
Values may be sent and summed in bfloat16 or wider, within the bound.
A program may use at most 128 MiB of HBM per device.

v0:
```python
import jax
import jax.numpy as jnp
from jax import lax
from jax.sharding import PartitionSpec as P


def silu_grad(preact, upstream):
    sigmoid_z = jax.nn.sigmoid(preact)
    return (upstream.astype(jnp.float32) * sigmoid_z * (1.0 + preact * (1.0 - sigmoid_z))).astype(
        jnp.bfloat16
    )


def spread_tiles(tiles, read_ids, write_ids, live_mask, panel, out_tiles, transpose):
    tile_size = tiles.shape[1]
    feat_width = panel.shape[-1]
    slots = tiles.shape[0]
    shaped = (
        tiles.reshape(4, slots // 4, tile_size, tile_size),
        read_ids.reshape(4, slots // 4),
        write_ids.reshape(4, slots // 4),
        live_mask.reshape(4, slots // 4),
    )
    form = "sji,sjf->sif" if transpose else "sij,sjf->sif"

    def step(total, block_data):
        part_tiles, read_part, write_part, live_part = block_data
        picked = panel[read_part]
        product = jnp.einsum(form, part_tiles, picked, preferred_element_type=jnp.float32)
        product = product * live_part.astype(jnp.float32)[:, None, None]
        return (total.at[write_part].add(product), None)

    start = jnp.zeros((out_tiles, tile_size, feat_width), jnp.float32)
    return lax.scan(step, start, shaped)[0]


def body(features, grad_out, weight, tiles, tile_row, tile_col, tile_count):
    segment = features.shape[0]
    feat_width = features.shape[1]
    tile_size = tiles.shape[1]
    mixed_rows = jnp.dot(features, weight, preferred_element_type=jnp.float32).astype(jnp.bfloat16)
    panel = lax.all_gather(mixed_rows, "row", axis=0, tiled=True)
    live_mask = jnp.arange(tile_row.shape[0], dtype=jnp.int32) < tile_count[0]
    col_tiles = panel.shape[0] // tile_size
    row_tiles = segment * lax.axis_size("col") // tile_size
    partial_value = spread_tiles(
        tiles,
        tile_col,
        tile_row,
        live_mask,
        panel.reshape(col_tiles, tile_size, feat_width),
        row_tiles,
        False,
    )
    partial_value = partial_value.reshape(row_tiles * tile_size, feat_width)
    owned = lax.psum_scatter(
        partial_value.astype(jnp.bfloat16), "col", scatter_dimension=0, tiled=True
    ).astype(jnp.float32)
    grad_block = lax.all_gather(silu_grad(owned, grad_out), "col", axis=0, tiled=True)
    back_terms = spread_tiles(
        tiles,
        tile_row,
        tile_col,
        live_mask,
        grad_block.reshape(row_tiles, tile_size, feat_width),
        col_tiles,
        True,
    )
    back_terms = back_terms.reshape(col_tiles * tile_size, feat_width).astype(jnp.bfloat16)
    summed = lax.psum_scatter(back_terms, "row", scatter_dimension=0, tiled=True).astype(
        jnp.float32
    )
    grad_panel = summed.astype(jnp.bfloat16)
    grad_features = lax.dot_general(
        grad_panel, weight, (((1,), (1,)), ((), ())), preferred_element_type=jnp.float32
    ).astype(jnp.bfloat16)
    local_weight = lax.dot_general(
        features, grad_panel, (((0,), (0,)), ((), ())), preferred_element_type=jnp.float32
    )
    grad_weight = lax.psum(local_weight, ("row", "col"))
    return (grad_features, grad_weight)


def solution(mesh):
    in_specs = (
        P(("row", "col"), None),
        P(("row", "col"), None),
        P(),
        P(("row", "col"), None, None),
        P(("row", "col")),
        P(("row", "col")),
        P(("row", "col")),
    )
    out_specs = (P(("row", "col"), None), P())
    return jax.shard_map(body, mesh=mesh, in_specs=in_specs, out_specs=out_specs, check_vma=False)
```

profile of v0, /device:TPU:0, one launch (start us, length us, event | category | flops | bytes accessed | tf_op | source)
XLA Modules:
  0.0 485.0 jit_solution(7939529680788866499)
XLA Ops:
  12.2 51.6 %all-gather.2.cloned.1.call-done = bf16[8192,256]{1,0:T(8,128)(2,1)} async-done(((bf16[512,256]{1,0:T(8,128)(2,1)}), bf16[8192,256]{1,0:T(8,128)(2,1)}) %all-gather.2.cloned.1.call-update) | async-done | bytes 4194320 | tf_op jit(solution)/shard_map/all_gather | solution.py:42
  63.9 81.0 %while.20 = (s32[]{:T(128)}, f32[8,128,256]{2,1,0:T(8,128)S(1)}, s32[4,48]{1,0:T(4,128)S(1)}, bf16[4,48,128,128]{3,2,1,0:T(8,128)(2,1)}, s32[4,48]{1,0:T(4,128)S...) while((s32[]{:T(128)}, f32[8,128,256]{2,1,0:T(8,128)S(1)}, ...), condition=%wide.region_2.3_spmd, body=%wide.region_0.2_spmd.sunk | while | flops 405800288 | bytes 36181848 | solution.py:34
  68.8 6.0 %broadcast_multiply_fusion.4 = f32[48,128,256]{2,1,0:T(8,128)} fusion(f32[48]{0:T(128)S(1)} %fusion.41, bf16[48,128,256]{2,1,0:T(8,128)(2,1)} %gather_fusion, bf16[4,48,128,128]{3,2,1,0:T(8,128)(2,1)} %get-tuple-element.232, s32[]{:T(128)S(6)} %copy.17), kind=kOutput, calls=%fused_computation.4.clone.1 | convolution fusion | flops 404226048 | bytes 11010244 | tf_op jit(solution)/shard_map/while/body/eval_jaxpr/sij,sjf->sif/dot_general | solution.py:29
  74.8 9.4 %scatter_fusion = f32[8,128,256]{2,1,0:T(8,128)S(1)} fusion(f32[8,128,256]{2,1,0:T(8,128)S(1)} %get-tuple-element.222, s32[48]{0:T(128)S(1)} %get-tuple-element.202, f32[48,128,256]{2,1,0:T(8,128)} %broadcast_multiply_fusion.4), kind=kCustom, calls=%fused_computation.2.clone.1 | custom fusion | flops 1572864 | bytes 18874560 | tf_op jit(solution)/shard_map/while/body/eval_jaxpr/scatter-add | solution.py:31
  89.0 6.0 %broadcast_multiply_fusion.4 = f32[48,128,256]{2,1,0:T(8,128)} fusion(f32[48]{0:T(128)S(1)} %fusion.41, bf16[48,128,256]{2,1,0:T(8,128)(2,1)} %gather_fusion, bf16[4,48,128,128]{3,2,1,0:T(8,128)(2,1)} %get-tuple-element.232, s32[]{:T(128)S(6)} %copy.17), kind=kOutput, calls=%fused_computation.4.clone.1 | convolution fusion | flops 404226048 | bytes 11010244 | tf_op jit(solution)/shard_map/while/body/eval_jaxpr/sij,sjf->sif/dot_general | solution.py:29
  95.0 9.4 %scatter_fusion = f32[8,128,256]{2,1,0:T(8,128)S(1)} fusion(f32[8,128,256]{2,1,0:T(8,128)S(1)} %get-tuple-element.222, s32[48]{0:T(128)S(1)} %get-tuple-element.202, f32[48,128,256]{2,1,0:T(8,128)} %broadcast_multiply_fusion.4), kind=kCustom, calls=%fused_computation.2.clone.1 | custom fusion | flops 1572864 | bytes 18874560 | tf_op jit(solution)/shard_map/while/body/eval_jaxpr/scatter-add | solution.py:31
  109.3 6.0 %broadcast_multiply_fusion.4 = f32[48,128,256]{2,1,0:T(8,128)} fusion(f32[48]{0:T(128)S(1)} %fusion.41, bf16[48,128,256]{2,1,0:T(8,128)(2,1)} %gather_fusion, bf16[4,48,128,128]{3,2,1,0:T(8,128)(2,1)} %get-tuple-element.232, s32[]{:T(128)S(6)} %copy.17), kind=kOutput, calls=%fused_computation.4.clone.1 | convolution fusion | flops 404226048 | bytes 11010244 | tf_op jit(solution)/shard_map/while/body/eval_jaxpr/sij,sjf->sif/dot_general | solution.py:29
  115.3 9.4 %scatter_fusion = f32[8,128,256]{2,1,0:T(8,128)S(1)} fusion(f32[8,128,256]{2,1,0:T(8,128)S(1)} %get-tuple-element.222, s32[48]{0:T(128)S(1)} %get-tuple-element.202, f32[48,128,256]{2,1,0:T(8,128)} %broadcast_multiply_fusion.4), kind=kCustom, calls=%fused_computation.2.clone.1 | custom fusion | flops 1572864 | bytes 18874560 | tf_op jit(solution)/shard_map/while/body/eval_jaxpr/scatter-add | solution.py:31
  129.5 6.0 %broadcast_multiply_fusion.4 = f32[48,128,256]{2,1,0:T(8,128)} fusion(f32[48]{0:T(128)S(1)} %fusion.41, bf16[48,128,256]{2,1,0:T(8,128)(2,1)} %gather_fusion, bf16[4,48,128,128]{3,2,1,0:T(8,128)(2,1)} %get-tuple-element.232, s32[]{:T(128)S(6)} %copy.17), kind=kOutput, calls=%fused_computation.4.clone.1 | convolution fusion | flops 404226048 | bytes 11010244 | tf_op jit(solution)/shard_map/while/body/eval_jaxpr/sij,sjf->sif/dot_general | solution.py:29
  135.5 9.4 %scatter_fusion = f32[8,128,256]{2,1,0:T(8,128)S(1)} fusion(f32[8,128,256]{2,1,0:T(8,128)S(1)} %get-tuple-element.222, s32[48]{0:T(128)S(1)} %get-tuple-element.202, f32[48,128,256]{2,1,0:T(8,128)} %broadcast_multiply_fusion.4), kind=kCustom, calls=%fused_computation.2.clone.1 | custom fusion | flops 1572864 | bytes 18874560 | tf_op jit(solution)/shard_map/while/body/eval_jaxpr/scatter-add | solution.py:31
  145.9 8.7 %copy.9 = bf16[192,128,128]{1,2,0:T(8,128)(2,1)} copy(bf16[192,128,128]{2,1,0:T(8,128)(2,1)} %bitcast.83) | data formatting | bytes 12582912 | tf_op args[3]
  160.3 8.6 %all_gather.7 = bf16[1024,256]{1,0:T(8,128)(2,1)S(1)} all-gather(bf16[512,256]{1,0:T(8,128)(2,1)S(1)} %fusion.21), channel_id=1, replica_groups=mesh['row'=16,'col'=2] {'col'}, dimensions={0}, use_global_device_ids=true | all-gather | bytes 786432 | tf_op jit(solution)/shard_map/all_gather | solution.py:59
  173.1 92.9 %while.21 = (s32[]{:T(128)}, f32[64,128,256]{2,1,0:T(8,128)}, s32[4,48]{1,0:T(4,128)S(1)}, bf16[4,48,128,128]{2,3,1,0:T(8,128)(2,1)}, s32[4,48]{1,0:T(4,128)S(1)...) while((s32[]{:T(128)}, f32[64,128,256]{2,1,0:T(8,128)}, ...), condition=%wide.region_6.7_spmd, body=%wide.region_4.6_spmd.sunk | while | flops 405800288 | bytes 36181848 | solution.py:34
  175.7 5.9 %broadcast_multiply_fusion.5 = f32[48,128,256]{2,1,0:T(8,128)} fusion(f32[48]{0:T(128)S(1)} %fusion.45, bf16[48,128,256]{2,1,0:T(8,128)(2,1)} %gather_fusion.1, bf16[4,48,128,128]{2,3,1,0:T(8,128)(2,1)} %get-tuple-element.256, s32[]{:T(128)S(6)} %copy.23), kind=kOutput, calls=%fused_computation.19.clone.1 | convolution fusion | flops 404226048 | bytes 11010244 | tf_op jit(solution)/shard_map/while/body/eval_jaxpr/sji,sjf->sif/dot_general | solution.py:29
  181.6 15.0 %scatter_fusion.1 = f32[64,128,256]{2,1,0:T(8,128)} fusion(f32[64,128,256]{2,1,0:T(8,128)} %get-tuple-element.246, s32[48]{0:T(128)S(1)} %get-tuple-element.211, f32[48,128,256]{2,1,0:T(8,128)} %broadcast_multiply_fusion.5), kind=kCustom, calls=%fused_computation.3.clone.1 | custom fusion | flops 1572864 | bytes 18874560 | tf_op jit(solution)/shard_map/while/body/eval_jaxpr/scatter-add | solution.py:31
  199.1 5.9 %broadcast_multiply_fusion.5 = f32[48,128,256]{2,1,0:T(8,128)} fusion(f32[48]{0:T(128)S(1)} %fusion.45, bf16[48,128,256]{2,1,0:T(8,128)(2,1)} %gather_fusion.1, bf16[4,48,128,128]{2,3,1,0:T(8,128)(2,1)} %get-tuple-element.256, s32[]{:T(128)S(6)} %copy.23), kind=kOutput, calls=%fused_computation.19.clone.1 | convolution fusion | flops 404226048 | bytes 11010244 | tf_op jit(solution)/shard_map/while/body/eval_jaxpr/sji,sjf->sif/dot_general | solution.py:29
  205.0 14.8 %scatter_fusion.1 = f32[64,128,256]{2,1,0:T(8,128)} fusion(f32[64,128,256]{2,1,0:T(8,128)} %get-tuple-element.246, s32[48]{0:T(128)S(1)} %get-tuple-element.211, f32[48,128,256]{2,1,0:T(8,128)} %broadcast_multiply_fusion.5), kind=kCustom, calls=%fused_computation.3.clone.1 | custom fusion | flops 1572864 | bytes 18874560 | tf_op jit(solution)/shard_map/while/body/eval_jaxpr/scatter-add | solution.py:31
  222.4 5.9 %broadcast_multiply_fusion.5 = f32[48,128,256]{2,1,0:T(8,128)} fusion(f32[48]{0:T(128)S(1)} %fusion.45, bf16[48,128,256]{2,1,0:T(8,128)(2,1)} %gather_fusion.1, bf16[4,48,128,128]{2,3,1,0:T(8,128)(2,1)} %get-tuple-element.256, s32[]{:T(128)S(6)} %copy.23), kind=kOutput, calls=%fused_computation.19.clone.1 | convolution fusion | flops 404226048 | bytes 11010244 | tf_op jit(solution)/shard_map/while/body/eval_jaxpr/sji,sjf->sif/dot_general | solution.py:29
  228.3 14.6 %scatter_fusion.1 = f32[64,128,256]{2,1,0:T(8,128)} fusion(f32[64,128,256]{2,1,0:T(8,128)} %get-tuple-element.246, s32[48]{0:T(128)S(1)} %get-tuple-element.211, f32[48,128,256]{2,1,0:T(8,128)} %broadcast_multiply_fusion.5), kind=kCustom, calls=%fused_computation.3.clone.1 | custom fusion | flops 1572864 | bytes 18874560 | tf_op jit(solution)/shard_map/while/body/eval_jaxpr/scatter-add | solution.py:31
  245.5 5.9 %broadcast_multiply_fusion.5 = f32[48,128,256]{2,1,0:T(8,128)} fusion(f32[48]{0:T(128)S(1)} %fusion.45, bf16[48,128,256]{2,1,0:T(8,128)(2,1)} %gather_fusion.1, bf16[4,48,128,128]{2,3,1,0:T(8,128)(2,1)} %get-tuple-element.256, s32[]{:T(128)S(6)} %copy.23), kind=kOutput, calls=%fused_computation.19.clone.1 | convolution fusion | flops 404226048 | bytes 11010244 | tf_op jit(solution)/shard_map/while/body/eval_jaxpr/sji,sjf->sif/dot_general | solution.py:29
  251.4 14.6 %scatter_fusion.1 = f32[64,128,256]{2,1,0:T(8,128)} fusion(f32[64,128,256]{2,1,0:T(8,128)} %get-tuple-element.246, s32[48]{0:T(128)S(1)} %get-tuple-element.211, f32[48,128,256]{2,1,0:T(8,128)} %broadcast_multiply_fusion.5), kind=kCustom, calls=%fused_computation.3.clone.1 | custom fusion | flops 1572864 | bytes 18874560 | tf_op jit(solution)/shard_map/while/body/eval_jaxpr/scatter-add | solution.py:31
  266.0 6.0 %convert_element_type.55 = bf16[64,128,256]{2,1,0:T(8,128)(2,1)} convert(f32[64,128,256]{2,1,0:T(8,128)} %get-tuple-element.77) | non-fusion elementwise | flops 2097152 | bytes 12582912 | tf_op jit(solution)/shard_map/convert_element_type | solution.py:69
  272.1 73.0 %reduce-scatter.5.cloned.1.call-done = bf16[512,256]{1,0:T(8,128)(2,1)} async-done(((bf16[8192,256]{1,0:T(8,128)(2,1)}), bf16[512,256]{1,0:T(8,128)(2,1)}) %reduce-scatter.5.cloned.1.call-update) | async-done | bytes 262160 | tf_op jit(solution)/shard_map/reduce_scatter | solution.py:70
  349.0 127.7 %all-reduce.2.cloned.1.call-done = f32[256,256]{0,1:T(8,128)} async-done(((f32[256,256]{0,1:T(8,128)}), f32[256,256]{0,1:T(8,128)}) %all-reduce.2.cloned.1.call-update) | async-done | bytes 262160 | tf_op jit(solution)/shard_map/psum | solution.py:80
  (58 shorter events, 50.6 us)
Async XLA Ops:
  7.2 1.0 copy-start
  7.2 56.7 %all-gather.2.cloned.1.call-start = ((), (), s32[]{:S(2)}) async-start(), calls=%async_computation.2 | async-start | bytes 4456448 | tf_op jit(solution)/shard_map/all_gather | solution.py:42
  10.0 149.2 %reduce-scatter.3.cloned.1.call-start = ((), (), s32[]{:S(2)}) async-start(), calls=%async_computation.3 | async-start | bytes 786432 | tf_op jit(solution)/shard_map/reduce_scatter | solution.py:56
  145.8 13.3 %copy-start.2 = (bf16[512,256]{1,0:T(8,128)(2,1)S(1)}, bf16[512,256]{1,0:T(8,128)(2,1)}, u32[]{:S(2)}) copy-start(bf16[512,256]{1,0:T(8,128)(2,1)} %param.12) | copy-start | bytes 786436
  145.8 199.3 %reduce-scatter.5.cloned.1.call-start = ((), (), s32[]{:S(2)}) async-start(), calls=%async_computation.4 | async-start | bytes 4456448 | tf_op jit(solution)/shard_map/reduce_scatter | solution.py:70
  266.0 81.0 %copy-start.1 = (bf16[256,256]{1,0:T(8,128)(2,1)S(1)}, bf16[256,256]{1,0:T(8,128)(2,1)}, u32[]{:S(2)}) copy-start(bf16[256,256]{1,0:T(8,128)(2,1)} %param.13) | copy-start | bytes 393220
  272.0 204.7 %all-reduce.2.cloned.1.call-start = ((), (), s32[]{:S(2)}) async-start(), calls=%async_computation.5 | async-start | bytes 524288 | tf_op jit(solution)/shard_map/psum | solution.py:80
Sparse Core Ops, SparseCore 0:
  10.7 53.0 all-gather.1
  145.9 13.1 reduce-scatter.2
  272.1 72.9 reduce-scatter.4
  351.0 125.5 all-reduce.1
where the time goes:
time: 486 us; the launch traced here: 485 us
  waiting for transfers between devices  257 us (53%)
  other arithmetic  105 us (22%)
  matrix products  53.2 us (11%)
  local copies, waits for them, and re-layouts  46.5 us (10%)
  between operations  14.5 us (3%)
  blocking collectives  8.57 us (2%)
    psum x1, waiting for transfers between devices, body(): grad_weight = lax.psum(local_weight, ('row', 'col'))  128 us
    scatter-add x8, other arithmetic, step(): return (total.at[write_part].add(product), None)  96.6 us
    reduce_scatter x1, waiting for transfers between devices, body(): lax.psum_scatter(back_terms, 'row', scatter_dimension=0, tiled=True)  73 us
    all_gather x1, waiting for transfers between devices, body(): panel = lax.all_gather(mixed_rows, 'row', axis=0, tiled=True)  51.6 us
    dot_general x8, matrix products, step(): jnp.einsum(form, part_tiles, picked, preferred_element_type=jnp.float32)  47.5 us
    gather x8, local copies, waits for them, and re-layouts, step(): picked = panel[read_part]  29.3 us
    unnamed x8, local copies, waits for them, and re-layouts  11.4 us
  transfers between devices with their start and end apart: 4, of which 4 were waited for; matrix products, arithmetic and copies ran while one was open for 2% of the time, Pallas kernels for 0%

commit v1 on v0

v1 whole, which is shorter than its diff:
```python
import functools

import jax
import jax.numpy as jnp
from jax import lax
from jax.experimental import pallas as pl
from jax.experimental.pallas import tpu as pltpu
from jax.sharding import PartitionSpec as P

CHUNK = 16
GROUP = 4


def silu_grad(preact, upstream):
    sigmoid_z = jax.nn.sigmoid(preact)
    return (upstream.astype(jnp.float32) * sigmoid_z * (1.0 + preact * (1.0 - sigmoid_z))).astype(
        jnp.bfloat16
    )


def spread_kernel(transpose, read_ids, write_ids, count_ref, tiles_hbm, panel_ref, out_ref, buf, acc, sems):
    slots, tile_size, _ = tiles_hbm.shape
    out_tiles = out_ref.shape[0] // tile_size
    chunks = slots // CHUNK
    count = count_ref[0]
    live_chunks = (count + CHUNK - 1) // CHUNK

    def fetch(chunk):
        part = pl.ds(chunk * CHUNK, CHUNK)
        return pltpu.make_async_copy(tiles_hbm.at[part], buf.at[part], sems.at[chunk])

    for chunk in range(chunks):

        @pl.when(chunk < live_chunks)
        def _():
            fetch(chunk).start()

    acc[...] = jnp.zeros_like(acc)
    contract = (((0,), (0,)), ((), ())) if transpose else (((1,), (0,)), ((), ()))

    def one(slot, keep):
        src = pl.multiple_of(read_ids[slot] * tile_size, tile_size)
        product = lax.dot_general(
            buf[slot], panel_ref[pl.ds(src, tile_size), :], contract, preferred_element_type=jnp.float32
        )
        return jnp.where(keep, product, 0.0) if keep is not None else product

    def add(slot, product):
        dst = pl.multiple_of(write_ids[slot] * tile_size, tile_size)
        acc[pl.ds(dst, tile_size), :] += product

    def chunk_step(chunk, carry):
        fetch(chunk).wait()
        base = chunk * CHUNK
        groups = jnp.minimum(count - base, CHUNK) // GROUP

        def group_step(group, carry):
            first = base + group * GROUP
            products = [one(first + k, None) for k in range(GROUP)]
            for k in range(GROUP):
                add(first + k, products[k])
            return carry

        lax.fori_loop(0, groups, group_step, 0)

        def tail_step(slot, carry):
            add(slot, one(slot, None))
            return carry

        lax.fori_loop(base + groups * GROUP, jnp.minimum(count, base + CHUNK), tail_step, 0)
        return carry

    lax.fori_loop(0, live_chunks, chunk_step, 0)

    def finish(tile, carry):
        part = pl.ds(pl.multiple_of(tile * tile_size, tile_size), tile_size)
        out_ref[part, :] = acc[part, :].astype(out_ref.dtype)
        return carry

    lax.fori_loop(0, out_tiles, finish, 0)


def spread_tiles(tiles, read_ids, write_ids, count, panel, out_rows, transpose):
    slots, tile_size, _ = tiles.shape
    feat_width = panel.shape[-1]
    return pl.pallas_call(
        functools.partial(spread_kernel, transpose),
        out_shape=jax.ShapeDtypeStruct((out_rows, feat_width), jnp.bfloat16),
        in_specs=[
            pl.BlockSpec(memory_space=pltpu.SMEM),
            pl.BlockSpec(memory_space=pltpu.SMEM),
            pl.BlockSpec(memory_space=pltpu.SMEM),
            pl.BlockSpec(memory_space=pl.ANY),
            pl.BlockSpec(memory_space=pltpu.VMEM),
        ],
        out_specs=pl.BlockSpec(memory_space=pltpu.VMEM),
        scratch_shapes=[
            pltpu.VMEM(tiles.shape, tiles.dtype),
            pltpu.VMEM((out_rows, feat_width), jnp.float32),
            pltpu.SemaphoreType.DMA((slots // CHUNK,)),
        ],
        compiler_params=pltpu.CompilerParams(vmem_limit_bytes=60 * 1024 * 1024),
        name="back" if transpose else "forth",
    )(read_ids, write_ids, count, tiles, panel)


def body(features, grad_out, weight, tiles, tile_row, tile_col, tile_count):
    segment = features.shape[0]
    mixed_rows = jnp.dot(features, weight, preferred_element_type=jnp.float32).astype(jnp.bfloat16)
    panel = lax.all_gather(mixed_rows, "row", axis=0, tiled=True)
    row_span = segment * lax.axis_size("col")
    partial_value = spread_tiles(tiles, tile_col, tile_row, tile_count, panel, row_span, False)
    owned = lax.psum_scatter(partial_value, "col", scatter_dimension=0, tiled=True).astype(jnp.float32)
    grad_block = lax.all_gather(silu_grad(owned, grad_out), "col", axis=0, tiled=True)
    back_terms = spread_tiles(tiles, tile_row, tile_col, tile_count, grad_block, panel.shape[0], True)
    summed = lax.psum_scatter(back_terms, "row", scatter_dimension=0, tiled=True).astype(jnp.float32)
    grad_panel = summed.astype(jnp.bfloat16)
    grad_features = lax.dot_general(
        grad_panel, weight, (((1,), (1,)), ((), ())), preferred_element_type=jnp.float32
    ).astype(jnp.bfloat16)
    local_weight = lax.dot_general(
        features, grad_panel, (((0,), (0,)), ((), ())), preferred_element_type=jnp.float32
    )
    grad_weight = lax.psum(local_weight, ("row", "col"))
    return (grad_features, grad_weight)


def solution(mesh):
    in_specs = (
        P(("row", "col"), None),
        P(("row", "col"), None),
        P(),
        P(("row", "col"), None, None),
        P(("row", "col")),
        P(("row", "col")),
        P(("row", "col")),
    )
    out_specs = (P(("row", "col"), None), P())
    return jax.shard_map(body, mesh=mesh, in_specs=in_specs, out_specs=out_specs, check_vma=False)
```

time: 486 us -> 332 us (0.68)
  other arithmetic: 105 us -> 1.17 us
  matrix products: 53.2 us -> 5.66 us
  local copies, waits for them, and re-layouts: 46.5 us -> 2.7 us
  waiting for transfers between devices: 257 us -> 284 us
  Pallas kernels: 0 us -> 15.2 us
    scatter-add x8 -> x0, other arithmetic: 96.6 us -> none  [step(): return (total.at[write_part].add(product), None)]
    dot_general x8 -> x0, matrix products: 47.5 us -> none  [step(): jnp.einsum(form, part_tiles, picked, preferred_element_type=jnp.float32)]
    gather x8 -> x0, local copies, waits for them, and re-layouts: 29.3 us -> none  [step(): picked = panel[read_part]]
    reduce_scatter x1, waiting for transfers between devices: 4.59 us -> 21.9 us  [body(): lax.psum_scatter(partial_value, 'col', scatter_dimension=0, tiled=True)]
    pallas_call x0 -> x2, Pallas kernels: none -> 15.2 us  [spread_tiles(): pl.pallas_call(functools.partial(spread_kernel, transpose), out_shape=jax...]
    unnamed x8 -> x7, local copies, waits for them, and re-layouts: 11.4 us -> 2.7 us
    reduce_scatter x1, waiting for transfers between devices: 73 us -> 81.4 us  [body(): lax.psum_scatter(back_terms, 'row', scatter_dimension=0, tiled=True)]
    convert_element_type x10 -> x0, other arithmetic: 6.89 us -> none  [the longest x1 5.98 us: body(): back_terms.reshape(col_tiles * tile_size, feat_width).astype(jnp.bfloat16)]
  transfers between devices with their start and end apart: 4 -> 4, of which waited for: 4 -> 4; matrix products, arithmetic and copies ran while one was open for 2% -> 1% of each run, Pallas kernels for 0% -> 0%
where the time goes in v1:
time: 332 us
  waiting for transfers between devices  284 us (86%)
  Pallas kernels  15.2 us (5%)
  between operations  14.5 us (4%)
  blocking collectives  8.63 us (3%)
  matrix products  5.66 us (2%)
    psum x1, waiting for transfers between devices, body(): grad_weight = lax.psum(local_weight, ('row', 'col'))  128 us
    reduce_scatter x1, waiting for transfers between devices, body(): lax.psum_scatter(back_terms, 'row', scatter_dimension=0, tiled=True)  81.4 us
    all_gather x1, waiting for transfers between devices, body(): panel = lax.all_gather(mixed_rows, 'row', axis=0, tiled=True)  53.2 us
    reduce_scatter x1, waiting for transfers between devices, body(): lax.psum_scatter(partial_value, 'col', scatter_dimension=0, tiled=True)  21.9 us
    pallas_call x2, Pallas kernels, spread_tiles(): pl.pallas_call(functools.partial(spread_kernel, transpose), out_shape=jax...  15.2 us
    all_gather x1, blocking collectives, body(): lax.all_gather(silu_grad(owned, grad_out), 'col', axis=0, tiled=True)  8.63 us
  transfers between devices with their start and end apart: 4, of which 4 were waited for; matrix products, arithmetic and copies ran while one was open for 1% of the time, Pallas kernels for 0%

profile of v1, /device:TPU:0, one launch (start us, length us, event | category | flops | bytes accessed | tf_op | source)
XLA Modules:
  0.0 332.2 jit_solution(8789968704959038971)
XLA Ops:
  7.2 0.0 copy-start
  7.2 0.0 all-gather.2.cloned.1.call-start
  7.2 0.9 copy-done
  8.1 1.8 convolution_convert_fusion.1
  9.9 0.0 all-gather.2.cloned.1.call-update
  10.0 0.0 reduce-scatter.3.cloned.1.call-start
  10.7 0.0 copy-start.2
  10.7 53.2 %all-gather.2.cloned.1.call-done.panel_ref = bf16[8192,256]{1,0:T(8,128)(2,1)} async-done(((bf16[512,256]{1,0:T(8,128)(2,1)}), bf16[8192,256]{1,0:T(8,128)(2,1)}) %all-gather.2.cloned.1.call-update) | async-done | bytes 4194320 | tf_op jit(solution)/shard_map/all_gather | solution.py:110
  63.8 7.0 %forth.1 = bf16[1024,256]{1,0:T(8,128)(2,1)} custom-call(s32[192]{0:T(256)} %write_ids.3, s32[192]{0:T(256)} %read_ids.3, s32[1]{0:T(128)S(6)} %copy.11.count_ref, bf16[192,128,128]{2,1,0:T(8,128)(2,1)} %tiles_hbm.3, bf16[8192,256]{1,0:T(8,128)(2,1)} %all-gather.2.cloned.1.call-done.panel_ref), custom_call_target="tpu_custom_call" | custom-call | tf_op jit(solution)/shard_map/forth/pallas_call | solution.py:86
  70.9 0.0 reduce-scatter.3.cloned.1.call-update
  70.9 0.0 reduce-scatter.5.cloned.1.call-start
  71.0 21.9 %reduce-scatter.3.cloned.1.call-done = bf16[512,256]{1,0:T(8,128)(2,1)} async-done(((bf16[1024,256]{1,0:T(8,128)(2,1)}), bf16[512,256]{1,0:T(8,128)(2,1)}) %reduce-scatter.3.cloned.1.call-update) | async-done | bytes 262160 | tf_op jit(solution)/shard_map/reduce_scatter | solution.py:113
  92.9 1.2 fusion.5
  94.1 8.6 %all_gather.7.panel_ref = bf16[1024,256]{1,0:T(8,128)(2,1)} all-gather(bf16[512,256]{1,0:T(8,128)(2,1)S(1)} %fusion.5), channel_id=1, replica_groups=mesh['row'=16,'col'=2] {'col'}, dimensions={0}, use_global_device_ids=true | all-gather | bytes 786432 | tf_op jit(solution)/shard_map/all_gather | solution.py:114
  102.7 8.1 %back.1 = bf16[8192,256]{1,0:T(8,128)(2,1)} custom-call(s32[192]{0:T(256)} %read_ids.3, s32[192]{0:T(256)} %write_ids.3, s32[1]{0:T(128)S(6)} %copy.11.count_ref, bf16[192,128,128]{2,1,0:T(8,128)(2,1)} %tiles_hbm.3, bf16[1024,256]{1,0:T(8,128)(2,1)} %all_gather.7.panel_ref), custom_call_target="tpu_custom_call" | custom-call | tf_op jit(solution)/shard_map/back/pallas_call | solution.py:86
  110.9 0.0 copy-start.1
  110.9 0.0 reduce-scatter.5.cloned.1.call-update
  110.9 0.0 all-reduce.2.cloned.1.call-start
  110.9 81.4 %reduce-scatter.5.cloned.1.call-done = bf16[512,256]{1,0:T(8,128)(2,1)} async-done(((bf16[8192,256]{1,0:T(8,128)(2,1)}), bf16[512,256]{1,0:T(8,128)(2,1)}) %reduce-scatter.5.cloned.1.call-update) | async-done | bytes 262160 | tf_op jit(solution)/shard_map/reduce_scatter | solution.py:116
  192.3 1.9 convolution_bitcast_fusion
  194.3 0.0 all-reduce.2.cloned.1.call-update
  194.3 1.9 convolution_convert_fusion
  196.2 127.7 %all-reduce.2.cloned.1.call-done = f32[256,256]{0,1:T(8,128)} async-done(((f32[256,256]{0,1:T(8,128)}), f32[256,256]{0,1:T(8,128)}) %all-reduce.2.cloned.1.call-update) | async-done | bytes 262160 | tf_op jit(solution)/shard_map/psum | solution.py:124
  323.9 1.8 copy.9
  (2 shorter events, 0.0 us)
Async XLA Ops:
  7.2 1.0 copy-start
  7.2 56.7 %all-gather.2.cloned.1.call-start = ((), (), s32[]{:S(2)}) async-start(), calls=%async_computation.2 | async-start | bytes 4456448 | tf_op jit(solution)/shard_map/all_gather | solution.py:110
  10.0 82.9 %reduce-scatter.3.cloned.1.call-start = ((), (), s32[]{:S(2)}) async-start(), calls=%async_computation.3 | async-start | bytes 786432 | tf_op jit(solution)/shard_map/reduce_scatter | solution.py:113
  10.7 82.2 %copy-start.2 = (bf16[512,256]{1,0:T(8,128)(2,1)S(1)}, bf16[512,256]{1,0:T(8,128)(2,1)}, u32[]{:S(2)}) copy-start(bf16[512,256]{1,0:T(8,128)(2,1)} %param.8) | copy-start | bytes 786436
  70.9 121.4 %reduce-scatter.5.cloned.1.call-start = ((), (), s32[]{:S(2)}) async-start(), calls=%async_computation.4 | async-start | bytes 4456448 | tf_op jit(solution)/shard_map/reduce_scatter | solution.py:116
  110.9 83.4 %copy-start.1 = (bf16[256,256]{1,0:T(8,128)(2,1)S(1)}, bf16[256,256]{1,0:T(8,128)(2,1)}, u32[]{:S(2)}) copy-start(bf16[256,256]{1,0:T(8,128)(2,1)} %param.9) | copy-start | bytes 393220
  110.9 213.0 %all-reduce.2.cloned.1.call-start = ((), (), s32[]{:S(2)}) async-start(), calls=%async_computation.5 | async-start | bytes 524288 | tf_op jit(solution)/shard_map/psum | solution.py:124
Sparse Core Ops, SparseCore 0:
  10.7 53.0 all-gather.1
  71.0 21.8 reduce-scatter.2
  111.0 81.2 reduce-scatter.4
  198.3 125.6 all-reduce.1

commit v2 on v1

--- a/solution.py
+++ b/solution.py
@@ -11,11 +11,444 @@
 GROUP = 4
 
 
+MESH = pl.DeviceIdType.MESH
+VMEM_SPEC = pl.BlockSpec(memory_space=pltpu.VMEM)
+LIMIT = 60 * 1024 * 1024
+
+
 def silu_grad(preact, upstream):
     sigmoid_z = jax.nn.sigmoid(preact)
     return (upstream.astype(jnp.float32) * sigmoid_z * (1.0 + preact * (1.0 - sigmoid_z))).astype(
         jnp.bfloat16
     )
+
+
+def ring_place(chip, chips):
+    half = lax.div(chip, 2)
+    return jnp.where(lax.rem(chip, 2) == 0, half, chips - 1 - half)
+
+
+def ring_chip(place, chips):
+    place = lax.rem(place + 2 * chips, chips)
+    return jnp.where(place < chips // 2, 2 * place, 2 * (chips - 1 - place) + 1)
+
+
+def row_device(chip, core):
+    return {"row": chip * 2 + core}
+
+
+def greet(partners):
+    barrier = pltpu.get_barrier_semaphore()
+    for partner in partners:
+        pl.semaphore_signal(barrier, inc=1, device_id=partner, device_id_type=MESH)
+    pl.semaphore_wait(barrier, len(partners))
+
+
+def remote(src, dst, send_sem, recv_sem, device):
+    return pltpu.make_async_remote_copy(
+        src_ref=src, dst_ref=dst, send_sem=send_sem, recv_sem=recv_sem, device_id=device, device_id_type=MESH
+    )
+
+
+def gather_kernel(n_row, f_ref, w_ref, fp_ref, mp_ref, ssem, rsem, xs, xr, os, orr):
+    chips = n_row // 2
+    seg = f_ref.shape[0]
+    half = seg // 2
+    me = lax.axis_index("row")
+    core = lax.rem(me, 2)
+    chip = lax.div(me, 2)
+    place = ring_place(chip, chips)
+    ways = (1, -1)
+    nexts = [row_device(ring_chip(place + way, chips), core) for way in ways]
+    sibling = row_device(chip, 1 - core)
+    greet(nexts + [sibling])
+    far = chips // 2
+    plans = [
+        [(h, k) for k in range(1, far) for h in (way, 1 - way)] + [(way, far)] for way in (0, 1)
+    ]
+    count = len(plans[0])
+
+    def rows_of(owner, h):
+        return pl.ds(pl.multiple_of(owner * seg + h * half, half), half)
+
+    def origin(way, k):
+        return ring_chip(place - ways[way] * k, chips)
+
+    def hop(way, i):
+        h, k = plans[way][i]
+        if k == 1:
+            src = f_ref.at[pl.ds(h * half, half)]
+            rows = rows_of(me, h)
+        else:
+            rows = rows_of(origin(way, k - 1) * 2 + core, h)
+            src = fp_ref.at[rows]
+        return remote(src, fp_ref.at[rows], ssem.at[way, i], rsem.at[way, i], nexts[way])
+
+    def across(way, i):
+        h, k = plans[way][i]
+        rows = rows_of(origin(way, k) * 2 + core, h)
+        return remote(fp_ref.at[rows], fp_ref.at[rows], xs.at[way, i], xr.at[way, i], sibling)
+
+    def own_across(h):
+        return remote(
+            f_ref.at[pl.ds(h * half, half)], fp_ref.at[rows_of(me, h)], os.at[h], orr.at[h], sibling
+        )
+
+    def mix(owner, h):
+        rows = rows_of(owner, h)
+        mp_ref[rows, :] = jnp.dot(
+            fp_ref[rows, :], w_ref[...], preferred_element_type=jnp.float32
+        ).astype(mp_ref.dtype)
+
+    for i in (0, 1):
+        for way in (0, 1):
+            hop(way, i).start()
+    for h in (0, 1):
+        own_across(h).start()
+    fp_ref[pl.ds(pl.multiple_of(me * seg, seg), seg), :] = f_ref[...]
+    for h in (0, 1):
+        mix(me, h)
+    for i in range(count):
+        for way in (0, 1):
+            hop(way, i).wait_recv()
+            if i + 2 < count:
+                hop(way, i + 2).start()
+            across(way, i).start()
+        if i == 0:
+            for h in (0, 1):
+                own_across(h).wait_recv()
+                mix(chip * 2 + 1 - core, h)
+        for way in (0, 1):
+            h, k = plans[way][i]
+            mix(origin(way, k) * 2 + core, h)
+            if i > 0:
+                h, k = plans[way][i - 1]
+                across(way, i - 1).wait_recv()
+                mix(origin(way, k) * 2 + 1 - core, h)
+    for way in (0, 1):
+        h, k = plans[way][count - 1]
+        across(way, count - 1).wait_recv()
+        mix(origin(way, k) * 2 + 1 - core, h)
+    for way in (0, 1):
+        for i in range(count):
+            hop(way, i).wait_send()
+            across(way, i).wait_send()
+    for h in (0, 1):
+        own_across(h).wait_send()
+
+
+def gather_mixed(features, weight, n_row):
+    seg, feat_width = features.shape
+    count = n_row // 2 - 1
+    shape = jax.ShapeDtypeStruct((n_row * seg, feat_width), features.dtype)
+    dma = pltpu.SemaphoreType.DMA
+    return pl.pallas_call(
+        functools.partial(gather_kernel, n_row),
+        out_shape=(shape, shape),
+        in_specs=[VMEM_SPEC] * 2,
+        out_specs=(VMEM_SPEC, VMEM_SPEC),
+        scratch_shapes=[dma((2, count))] * 4 + [dma((2,))] * 2,
+        compiler_params=pltpu.CompilerParams(
+            collective_id=0, has_side_effects=True, vmem_limit_bytes=LIMIT
+        ),
+        name="gather",
+    )(features, weight)
+
+
+PARTS = 4
+
+
+def exchange_kernel(n_col, part_ref, up_ref, out_ref, inbox, ssem, rsem, gs, gr):
+    seg = up_ref.shape[0]
+    step = seg // PARTS
+    me = lax.axis_index("col")
+    others = [lax.rem(me + o, n_col) for o in range(1, n_col)]
+    greet([{"col": other} for other in others])
+
+    def rows_of(owner, c):
+        return pl.ds(pl.multiple_of(owner * seg + c * step, step), step)
+
+    def there(o, c):
+        return remote(
+            part_ref.at[rows_of(others[o], c)],
+            inbox.at[o, pl.ds(c * step, step)],
+            ssem.at[o, c],
+            rsem.at[o, c],
+            {"col": others[o]},
+        )
+
+    def back(o, c):
+        rows = rows_of(me, c)
+        return remote(out_ref.at[rows], out_ref.at[rows], gs.at[o, c], gr.at[o, c], {"col": others[o]})
+
+    for c in range(PARTS):
+        for o in range(n_col - 1):
+            there(o, c).start()
+    for c in range(PARTS):
+        rows = rows_of(me, c)
+        total = part_ref[rows, :].astype(jnp.float32)
+        for o in range(n_col - 1):
+            there(o, c).wait_recv()
+            total = total + inbox[o, pl.ds(c * step, step), :].astype(jnp.float32)
+        out_ref[rows, :] = silu_grad(total, up_ref[pl.ds(c * step, step), :])
+        for o in range(n_col - 1):
+            back(o, c).start()
+    for c in range(PARTS):
+        for o in range(n_col - 1):
+            back(o, c).wait_recv()
+    for c in range(PARTS):
+        for o in range(n_col - 1):
+            there(o, c).wait_send()
+            back(o, c).wait_send()
+
+
+def exchange(partial_value, grad_out, n_col):
+    seg, feat_width = grad_out.shape
+    dma = pltpu.SemaphoreType.DMA
+    return pl.pallas_call(
+        functools.partial(exchange_kernel, n_col),
+        out_shape=jax.ShapeDtypeStruct(partial_value.shape, jnp.bfloat16),
+        in_specs=[VMEM_SPEC] * 2,
+        out_specs=VMEM_SPEC,
+        scratch_shapes=[pltpu.VMEM((n_col - 1, seg, feat_width), jnp.bfloat16)]
+        + [dma((n_col - 1, PARTS))] * 4,
+        compiler_params=pltpu.CompilerParams(
+            collective_id=1, has_side_effects=True, vmem_limit_bytes=LIMIT
+        ),
+        name="exchange",
+    )(partial_value, grad_out)
+
+
+def scatter_kernel(
+    n_row, n_col, back_ref, fp_hbm, w_ref, gf_ref, gw_ref, fp_ref, xbuf, xown, sbuf, rbuf,
+    gsum, gsib_out, gsib_in, gout, gin, gcol, gslice, gfin,
+    fsem, ssem, rsem, xs, xr, os, orr, ga, gb_s, gb_r, gc_s, gc_r, gd_s, gd_r, ge,
+):
+    chips = n_row // 2
+    seg = gf_ref.shape[0]
+    half = seg // 2
+    me = lax.axis_index("row")
+    mycol = lax.axis_index("col")
+    core = lax.rem(me, 2)
+    chip = lax.div(me, 2)
+    place = ring_place(chip, chips)
+    ways = (1, -1)
+    nexts = [row_device(ring_chip(place + way, chips), core) for way in ways]
+    sibling = row_device(chip, 1 - core)
+    peers = [row_device(lax.rem(chip + o, chips), core) for o in range(1, chips)]
+    cols = [{"col": lax.rem(mycol + o, n_col)} for o in range(1, n_col)]
+    width = gw_ref.shape[1]
+    rows_each = gw_ref.shape[0] // 2 // chips
+    load = pltpu.make_async_copy(fp_hbm, fp_ref, fsem)
+    load.start()
+    greet(peers + [sibling] + cols)
+    far = chips // 2
+    plans = [
+        [(way, far)] + [(h, k) for k in range(far - 1, 0, -1) for h in (1 - way, way)]
+        for way in (0, 1)
+    ]
+    count = len(plans[0])
+
+    def rows_of(owner, h):
+        return pl.ds(pl.multiple_of(owner * seg + h * half, half), half)
+
+    def target(way, i):
+        h, k = plans[way][i]
+        return ring_chip(place + ways[way] * k, chips), h
+
+    def across(way, i):
+        to, h = target(way, i)
+        return remote(
+            back_ref.at[rows_of(to * 2 + 1 - core, h)], xbuf.at[way, i], xs.at[way, i], xr.at[way, i], sibling
+        )
+
+    def own_across(h):
+        return remote(
+            back_ref.at[rows_of(chip * 2 + 1 - core, h)], xown.at[h], os.at[h], orr.at[h], sibling
+        )
+
+    def hop(way, i):
+        return remote(sbuf.at[way, i], rbuf.at[way, i], ssem.at[way, i], rsem.at[way, i], nexts[way])
+
+    def step(way, i):
+        to, h = target(way, i)
+        across(way, i).wait_recv()
+        total = back_ref[rows_of(to * 2 + core, h), :].astype(jnp.float32) + xbuf[way, i].astype(jnp.float32)
+        if i >= 2:
+            hop(way, i - 2).wait_recv()
+            total = total + rbuf[way, i - 2].astype(jnp.float32)
+        sbuf[way, i] = total.astype(sbuf.dtype)
+        hop(way, i).start()
+
+    for i in range(count):
+        for way in (0, 1):
+            across(way, i).start()
+    for h in (0, 1):
+        own_across(h).start()
+    for i in (0, 1):
+        for way in (0, 1):
+            step(way, i)
+
+    load.wait()
+    gsum[...] = jnp.zeros_like(gsum)
+
+    @pl.loop(0, n_row)
+    def _(block):
+        rows = pl.ds(pl.multiple_of(block * seg, seg), seg)
+        gsum[...] += lax.dot_general(
+            fp_ref[rows, :], back_ref[rows, :], (((0,), (0,)), ((), ())), preferred_element_type=jnp.float32
+        )
+
+    own_rows = gw_ref.shape[0] // 2
+
+    def half_rows(which):
+        return pl.ds(pl.multiple_of(which * own_rows, own_rows), own_rows)
+
+    gsib_out[...] = gsum[half_rows(1 - core), :].astype(gsib_out.dtype)
+    sib_copy = remote(gsib_out, gsib_in, ga.at[0], ga.at[1], sibling)
+    sib_copy.start()
+
+    def spread(o):
+        return remote(
+            gout.at[lax.rem(chip + o, chips)], gin.at[o - 1], gb_s.at[o - 1], gb_r.at[o - 1], peers[o - 1]
+        )
+
+    def stage_b():
+        sib_copy.wait_recv()
+        total = gsum[half_rows(core), :] + gsib_in[...].astype(jnp.float32)
+        gsum[half_rows(core), :] = total
+        gout[...] = total.astype(gout.dtype).reshape(gout.shape)
+        for o in range(1, chips):
+            spread(o).start()
+
+    def over_cols(o):
+        return remote(gslice.at[0], gcol.at[o - 1], gc_s.at[o - 1], gc_r.at[o - 1], cols[o - 1])
+
+    def stage_c():
+        mine = pl.multiple_of(core * own_rows + chip * rows_each, rows_each)
+        total = gsum[pl.ds(mine, rows_each), :]
+        for o in range(1, chips):
+            spread(o).wait_recv()
+            total = total + gin[o - 1].astype(jnp.float32)
+        gslice[0] = total
+        for o in range(1, n_col):
+            over_cols(o).start()
+
+    def collect(o):
+        return remote(gslice.at[1], gfin.at[core, chip], gd_s.at[o - 1], gd_r.at[o - 1], peers[o - 1])
+
+    def stage_d():
+        total = gslice[0]
+        for o in range(1, n_col):
+            over_cols(o).wait_recv()
+        ordered = None
+        for c in range(n_col):
+            term = total
+            for o in range(1, n_col):
+                term = jnp.where(lax.rem(mycol - o + n_col, n_col) == c, gcol[o - 1], term)
+            ordered = term if ordered is None else ordered + term
+        gslice[1] = ordered
+        gfin[core, chip] = ordered
+        for o in range(1, chips):
+            collect(o).start()
+
+    last_copy = remote(gfin.at[core], gfin.at[core], ge.at[0], ge.at[1], sibling)
+
+    def stage_e():
+        for o in range(1, chips):
+            collect(o).wait_recv()
+        last_copy.start()
+
+    stages = {2: stage_b, 4: stage_c, 5: stage_d}
+    for i in range(2, count):
+        for way in (0, 1):
+            step(way, i)
+        if i in stages:
+            stages[i]()
+    for h in (0, 1):
+        own_across(h).wait_recv()
+    stage_e()
+    order = [count - 2, count - 1]
+    for h in (1, 0):
+        total = back_ref[rows_of(me, h), :].astype(jnp.float32) + xown[h].astype(jnp.float32)
+        for way in (0, 1):
+            for i in order:
+                if plans[way][i][0] == h:
+                    hop(way, i).wait_recv()
+                    total = total + rbuf[way, i].astype(jnp.float32)
+        gf_ref[pl.ds(h * half, half), :] = lax.dot_general(
+            total.astype(jnp.bfloat16), w_ref[...], (((1,), (1,)), ((), ())), preferred_element_type=jnp.float32
+        ).astype(gf_ref.dtype)
+    last_copy.wait_recv()
+    gw_ref[...] = gfin[...].reshape(gw_ref.shape)
+    for way in (0, 1):
+        for i in range(count):
+            hop(way, i).wait_send()
+            across(way, i).wait_send()
+    for h in (0, 1):
+        own_across(h).wait_send()
+    sib_copy.wait_send()
+    for o in range(1, chips):
+        spread(o).wait_send()
+        collect(o).wait_send()
+    for o in range(1, n_col):
+        over_cols(o).wait_send()
+    last_copy.wait_send()
+
+
+def scatter_sum(back_terms, feature_panel, weight, n_row, n_col):
+    rows, feat_width = back_terms.shape
+    seg = rows // n_row
+    half = seg // 2
+    chips = n_row // 2
+    count = chips - 1
+    in_width, out_width = weight.shape
+    each = in_width // 2 // chips
+    dma = pltpu.SemaphoreType.DMA
+    bf16, f32 = jnp.bfloat16, jnp.float32
+    return pl.pallas_call(
+        functools.partial(scatter_kernel, n_row, n_col),
+        out_shape=(
+            jax.ShapeDtypeStruct((seg, in_width), bf16),
+            jax.ShapeDtypeStruct((in_width, out_width), f32),
+        ),
+        in_specs=[VMEM_SPEC, pl.BlockSpec(memory_space=pl.ANY), VMEM_SPEC],
+        out_specs=(VMEM_SPEC, VMEM_SPEC),
+        scratch_shapes=[
+            pltpu.VMEM(feature_panel.shape, bf16),
+            pltpu.VMEM((2, count, half, feat_width), bf16),
+            pltpu.VMEM((2, half, feat_width), bf16),
+            pltpu.VMEM((2, count, half, feat_width), bf16),
+            pltpu.VMEM((2, count, half, feat_width), bf16),
+            pltpu.VMEM((in_width, out_width), f32),
+            pltpu.VMEM((in_width // 2, out_width), bf16),
+            pltpu.VMEM((in_width // 2, out_width), bf16),
+            pltpu.VMEM((chips, each, out_width), bf16),
+            pltpu.VMEM((chips - 1, each, out_width), bf16),
+            pltpu.VMEM((n_col - 1, each, out_width), f32),
+            pltpu.VMEM((2, each, out_width), f32),
+            pltpu.VMEM((2, chips, each, out_width), f32),
+            dma,
+            dma((2, count)),
+            dma((2, count)),
+            dma((2, count)),
+            dma((2, count)),
+            dma((2,)),
+            dma((2,)),
+            dma((2,)),
+            dma((chips - 1,)),
+            dma((chips - 1,)),
+            dma((n_col - 1,)),
+            dma((n_col - 1,)),
+            dma((chips - 1,)),
+            dma((chips - 1,)),
+            dma((2,)),
+        ],
+        compiler_params=pltpu.CompilerParams(
+            collective_id=2, has_side_effects=True, vmem_limit_bytes=LIMIT
+        ),
+        name="scatter",
+    )(back_terms, feature_panel, weight)
 
 
 def spread_kernel(transpose, read_ids, write_ids, count_ref, tiles_hbm, panel_ref, out_ref, buf, acc, sems):
@@ -99,30 +532,19 @@
             pltpu.VMEM((out_rows, feat_width), jnp.float32),
             pltpu.SemaphoreType.DMA((slots // CHUNK,)),
         ],
-        compiler_params=pltpu.CompilerParams(vmem_limit_bytes=60 * 1024 * 1024),
+        compiler_params=pltpu.CompilerParams(vmem_limit_bytes=LIMIT),
         name="back" if transpose else "forth",
     )(read_ids, write_ids, count, tiles, panel)
 
 
 def body(features, grad_out, weight, tiles, tile_row, tile_col, tile_count):
     segment = features.shape[0]
-    mixed_rows = jnp.dot(features, weight, preferred_element_type=jnp.float32).astype(jnp.bfloat16)
-    panel = lax.all_gather(mixed_rows, "row", axis=0, tiled=True)
-    row_span = segment * lax.axis_size("col")
-    partial_value = spread_tiles(tiles, tile_col, tile_row, tile_count, panel, row_span, False)
-    owned = lax.psum_scatter(partial_value, "col", scatter_dimension=0, tiled=True).astype(jnp.float32)
-    grad_block = lax.all_gather(silu_grad(owned, grad_out), "col", axis=0, tiled=True)
-    back_terms = spread_tiles(tiles, tile_row, tile_col, tile_count, grad_block, panel.shape[0], True)
-    summed = lax.psum_scatter(back_terms, "row", scatter_dimension=0, tiled=True).astype(jnp.float32)
-    grad_panel = summed.astype(jnp.bfloat16)
-    grad_features = lax.dot_general(
-        grad_panel, weight, (((1,), (1,)), ((), ())), preferred_element_type=jnp.float32
-    ).astype(jnp.bfloat16)
-    local_weight = lax.dot_general(
-        features, grad_panel, (((0,), (0,)), ((), ())), preferred_element_type=jnp.float32
-    )
-    grad_weight = lax.psum(local_weight, ("row", "col"))
-    return (grad_features, grad_weight)
+    n_row, n_col = lax.axis_size("row"), lax.axis_size("col")
+    feature_panel, panel = gather_mixed(features, weight, n_row)
+    partial_value = spread_tiles(tiles, tile_col, tile_row, tile_count, panel, segment * n_col, False)
+    grad_block = exchange(partial_value, grad_out, n_col)
+    back_terms = spread_tiles(tiles, tile_row, tile_col, tile_count, grad_block, segment * n_row, True)
+    return scatter_sum(back_terms, feature_panel, weight, n_row, n_col)
 
 
 def solution(mesh):

time: 332 us -> 112 us (0.34)
  waiting for transfers between devices: 284 us -> 0 us
  Pallas kernels: 15.2 us -> 108 us
  between operations: 14.5 us -> 1.32 us
  blocking collectives: 8.63 us -> 0 us
  matrix products: 5.66 us -> 0 us
    psum x1 -> x0, waiting for transfers between devices: 128 us -> none  [body(): grad_weight = lax.psum(local_weight, ('row', 'col'))]
    reduce_scatter x2 -> x0, waiting for transfers between devices: 103 us -> none  [the longest x1 81.4 us: body(): lax.psum_scatter(back_terms, 'row', scatter_dimension=0, tiled=True)]
    pallas_call x0 -> x3, Pallas kernels: none -> 95.4 us  [the longest x1 40.4 us: scatter_sum(): pl.pallas_call(functools.partial(scatter_kernel, n_row, n_col), out_shape...]
    all_gather x1 -> x0, waiting for transfers between devices: 53.2 us -> none  [body(): panel = lax.all_gather(mixed_rows, 'row', axis=0, tiled=True)]
    all_gather x1 -> x0, blocking collectives: 8.63 us -> none  [body(): lax.all_gather(silu_grad(owned, grad_out), 'col', axis=0, tiled=True)]
    dot_general x3 -> x0, matrix products: 5.66 us -> none  [the longest x1 1.92 us: body(): lax.dot_general(features, grad_panel, (((0,), (0,)), ((), ())), preferred...]
  transfers between devices with their start and end apart: 4 -> 0, of which waited for: 4 -> 0; matrix products, arithmetic and copies ran while one was open for 1% -> 0% of each run, Pallas kernels for 0% -> 0%
where the time goes in v2:
time: 112 us; the launch traced here: 113 us
  Pallas kernels  108 us (96%)
  local copies, waits for them, and re-layouts  3.34 us (3%)
  between operations  1.32 us (1%)
    pallas_call x1, Pallas kernels, scatter_sum(): pl.pallas_call(functools.partial(scatter_kernel, n_row, n_col), out_shape...  40.4 us
    pallas_call x1, Pallas kernels, gather_mixed(): pl.pallas_call(functools.partial(gather_kernel, n_row), out_shape=(shape,...  30.8 us
    pallas_call x1, Pallas kernels, exchange(): pl.pallas_call(functools.partial(exchange_kernel, n_col), out_shape=jax.S...  24.1 us
    pallas_call x2, Pallas kernels, spread_tiles(): pl.pallas_call(functools.partial(spread_kernel, transpose), out_shape=jax...  12.7 us
    unnamed x2, local copies, waits for them, and re-layouts  3.34 us

profile of v2, /device:TPU:0, one launch (start us, length us, event | category | flops | bytes accessed | tf_op | source)
XLA Modules:
  0.0 112.7 jit_solution(10188539394134781339)
XLA Ops:
  1.3 30.8 %gather.1 = (bf16[8192,256]{1,0:T(8,128)(2,1)}, bf16[8192,256]{1,0:T(8,128)(2,1)}) custom-call(bf16[512,256]{1,0:T(8,128)(2,1)} %f_ref.1, bf16[256,256]{1,0:T(8,128)(2,1)} %w_ref.3), custom_call_target="tpu_custom_call" | custom-call | tf_op jit(solution)/shard_map/gather/pallas_call | solution.py:145
  32.1 5.9 %forth.1.part_ref = bf16[1024,256]{1,0:T(8,128)(2,1)} custom-call(s32[192]{0:T(256)} %write_ids.3, s32[192]{0:T(256)} %read_ids.3, s32[1]{0:T(128)S(6)} %copy.11.count_ref, bf16[192,128,128]{2,1,0:T(8,128)(2,1)} %tiles_hbm.3, bf16[8192,256]{1,0:T(8,128)(2,1)} %get-tuple-element.4.panel_ref), custom_call_target="tpu_custom_call" | custom-call | tf_op jit(solution)/shard_map/forth/pallas_call | solution.py:519
  38.1 24.1 %exchange.1.panel_ref = bf16[1024,256]{1,0:T(8,128)(2,1)} custom-call(bf16[1024,256]{1,0:T(8,128)(2,1)} %forth.1.part_ref, bf16[512,256]{1,0:T(8,128)(2,1)} %up_ref.1), custom_call_target="tpu_custom_call" | custom-call | tf_op jit(solution)/shard_map/exchange/pallas_call | solution.py:208
  62.2 6.8 %back.1.back_ref = bf16[8192,256]{1,0:T(8,128)(2,1)} custom-call(s32[192]{0:T(256)} %read_ids.3, s32[192]{0:T(256)} %write_ids.3, s32[1]{0:T(128)S(6)} %copy.11.count_ref, bf16[192,128,128]{2,1,0:T(8,128)(2,1)} %tiles_hbm.3, bf16[1024,256]{1,0:T(8,128)(2,1)} %exchange.1.panel_ref), custom_call_target="tpu_custom_call" | custom-call | tf_op jit(solution)/shard_map/back/pallas_call | solution.py:519
  69.0 40.4 %scatter.1 = (bf16[512,256]{1,0:T(8,128)(2,1)}, f32[256,256]{1,0:T(8,128)}) custom-call(bf16[8192,256]{1,0:T(8,128)(2,1)} %back.1.back_ref, bf16[8192,256]{1,0:T(8,128)(2,1)} %get-tuple-element.5.fp_hbm, bf16[256,256]{1,0:T(8,128)(2,1)} %w_ref.3), custom_call_target="tpu_custom_call" | custom-call | tf_op jit(solution)/shard_map/scatter/pallas_call | solution.py:409
  109.4 1.7 %copy.12 = bf16[512,256]{1,0:T(8,128)(2,1)} copy(bf16[512,256]{1,0:T(8,128)(2,1)} %get-tuple-element.8) | data formatting | bytes 524288
  111.0 1.7 %copy.13 = f32[256,256]{1,0:T(8,128)} copy(f32[256,256]{1,0:T(8,128)} %get-tuple-element.9) | data formatting | bytes 524288

commit v3 on v2

--- a/solution.py
+++ b/solution.py
@@ -7,13 +7,15 @@
 from jax.experimental.pallas import tpu as pltpu
 from jax.sharding import PartitionSpec as P
 
-CHUNK = 16
-GROUP = 4
+GROUP = 8
 
 
 MESH = pl.DeviceIdType.MESH
 VMEM_SPEC = pl.BlockSpec(memory_space=pltpu.VMEM)
-LIMIT = 60 * 1024 * 1024
+
+
+def grant(bytes_held):
+    return bytes_held + 6 * 1024 * 1024
 
 
 def silu_grad(preact, upstream):
@@ -50,7 +52,46 @@
     )
 
 
-def gather_kernel(n_row, f_ref, w_ref, fp_ref, mp_ref, ssem, rsem, xs, xr, os, orr):
+def pair_plan(read_row, write_row, count, width):
+    f32 = jnp.float32
+    slots = read_row.shape[1]
+    lane = lax.broadcasted_iota(jnp.int32, (slots, slots), 1)
+    sub = lax.broadcasted_iota(jnp.int32, (slots, slots), 0)
+
+    def as_column(row):
+        return jnp.sum(jnp.where(lane == sub, row, 0.0), axis=1, keepdims=True)
+
+    read_col = as_column(jnp.broadcast_to(read_row.astype(f32), (slots, slots)))
+    row = jnp.broadcast_to(write_row.astype(f32), (slots, slots))
+    write_col = as_column(row)
+    col = jnp.broadcast_to(write_col, (slots, slots))
+    live = jnp.where((lane < count) & (sub < count), 1.0, 0.0)
+    same = jnp.where(row == col, live, 0.0)
+    rank_col = jnp.sum(jnp.where(lane < sub, same, 0.0), axis=1, keepdims=True)
+    rank_row = jnp.sum(jnp.where(sub < lane, same, 0.0), axis=0, keepdims=True)
+    odd_row = rank_row - 2.0 * jnp.floor(rank_row * 0.5)
+    opens = jnp.where(lane < count, 1.0 - jnp.broadcast_to(odd_row, (slots, slots)), 0.0)
+    base = jnp.sum(jnp.where(row < col, opens, 0.0), axis=1, keepdims=True)
+    pairs = jnp.sum(opens, axis=1, keepdims=True)[0:1, :]
+    place = lax.broadcasted_iota(jnp.int32, (slots, width), 1).astype(f32)
+    slot = lax.broadcasted_iota(jnp.int32, (slots, width), 0)
+    hit = jnp.where(slot < count, jnp.where(place == 2.0 * base + rank_col, 1.0, 0.0), 0.0)
+    slot_at = jnp.sum(hit * (slot - slots).astype(f32), axis=0, keepdims=True) + float(slots)
+    last = lax.broadcasted_iota(jnp.int32, (1, width), 1) == width - 1
+    slot_at = jnp.where(last, jnp.broadcast_to(pairs, (1, width)), slot_at)
+    read_at = jnp.sum(hit * read_col, axis=0, keepdims=True)
+    write_at = jnp.sum(hit * write_col, axis=0, keepdims=True)
+    return [part.astype(jnp.int32) for part in (slot_at, read_at, write_at)]
+
+
+def gather_kernel(
+    n_row, count_ref, f_ref, w_ref, tr_ref, tc_ref, tiles_hbm,
+    fp_ref, mp_ref, tiles_ref, forth_ref, back_ref,
+    ssem, rsem, xs, xr, os, orr, tsem,
+):
+    slots = tiles_hbm.shape[0]
+    load = pltpu.make_async_copy(tiles_hbm, tiles_ref.at[pl.ds(0, slots)], tsem)
+    load.start()
     chips = n_row // 2
     seg = f_ref.shape[0]
     half = seg // 2
@@ -108,6 +149,11 @@
     fp_ref[pl.ds(pl.multiple_of(me * seg, seg), seg), :] = f_ref[...]
     for h in (0, 1):
         mix(me, h)
+    tiles_ref[slots] = jnp.zeros_like(tiles_ref[slots])
+    tr, tc, live = tr_ref[...], tc_ref[...], count_ref[0]
+    for plan_ref, reads, writes in ((forth_ref, tc, tr), (back_ref, tr, tc)):
+        for line, part in enumerate(pair_plan(reads, writes, live, plan_ref.shape[1])):
+            plan_ref[line : line + 1, :] = part
     for i in range(count):
         for way in (0, 1):
             hop(way, i).wait_recv()
@@ -135,24 +181,33 @@
             across(way, i).wait_send()
     for h in (0, 1):
         own_across(h).wait_send()
-
-
-def gather_mixed(features, weight, n_row):
+    load.wait()
+
+
+def gather_mixed(features, weight, tiles, tile_row, tile_col, tile_count, n_row):
     seg, feat_width = features.shape
     count = n_row // 2 - 1
+    slots, tile_size, _ = tiles.shape
     shape = jax.ShapeDtypeStruct((n_row * seg, feat_width), features.dtype)
+    entries = slots + min(slots, n_row * seg // tile_size) + 2 * GROUP + 1
+    plan = jax.ShapeDtypeStruct((3, -(-entries // 128) * 128), jnp.int32)
+    held = jax.ShapeDtypeStruct((slots + 1, tile_size, tile_size), tiles.dtype)
     dma = pltpu.SemaphoreType.DMA
     return pl.pallas_call(
         functools.partial(gather_kernel, n_row),
-        out_shape=(shape, shape),
-        in_specs=[VMEM_SPEC] * 2,
-        out_specs=(VMEM_SPEC, VMEM_SPEC),
-        scratch_shapes=[dma((2, count))] * 4 + [dma((2,))] * 2,
+        out_shape=(shape, shape, held, plan, plan),
+        in_specs=[pl.BlockSpec(memory_space=pltpu.SMEM)]
+        + [VMEM_SPEC] * 4
+        + [pl.BlockSpec(memory_space=pltpu.MemorySpace.HBM)],
+        out_specs=(VMEM_SPEC,) * 5,
+        scratch_shapes=[dma((2, count))] * 4 + [dma((2,))] * 2 + [dma],
         compiler_params=pltpu.CompilerParams(
-            collective_id=0, has_side_effects=True, vmem_limit_bytes=LIMIT
+            collective_id=0,
+            has_side_effects=True,
+            vmem_limit_bytes=grant(4 * shape.size + 2 * held.size + 2 * features.size),
         ),
         name="gather",
-    )(features, weight)
+    )(tile_count, features, weight, tile_row.reshape(1, slots), tile_col.reshape(1, slots), tiles)
 
 
 PARTS = 4
@@ -213,16 +268,16 @@
         scratch_shapes=[pltpu.VMEM((n_col - 1, seg, feat_width), jnp.bfloat16)]
         + [dma((n_col - 1, PARTS))] * 4,
         compiler_params=pltpu.CompilerParams(
-            collective_id=1, has_side_effects=True, vmem_limit_bytes=LIMIT
+            collective_id=1, has_side_effects=True, vmem_limit_bytes=grant(6 * partial_value.size)
         ),
         name="exchange",
     )(partial_value, grad_out)
 
 
 def scatter_kernel(
-    n_row, n_col, back_ref, fp_hbm, w_ref, gf_ref, gw_ref, fp_ref, xbuf, xown, sbuf, rbuf,
+    n_row, n_col, back_ref, fp_ref, w_ref, gf_ref, gw_ref, xbuf, xown, sbuf, rbuf,
     gsum, gsib_out, gsib_in, gout, gin, gcol, gslice, gfin,
-    fsem, ssem, rsem, xs, xr, os, orr, ga, gb_s, gb_r, gc_s, gc_r, gd_s, gd_r, ge,
+    ssem, rsem, xs, xr, os, orr, ga, gb_s, gb_r, gc_s, gc_r, gd_s, gd_r, ge,
 ):
     chips = n_row // 2
     seg = gf_ref.shape[0]
@@ -239,8 +294,6 @@
     cols = [{"col": lax.rem(mycol + o, n_col)} for o in range(1, n_col)]
     width = gw_ref.shape[1]
     rows_each = gw_ref.shape[0] // 2 // chips
-    load = pltpu.make_async_copy(fp_hbm, fp_ref, fsem)
-    load.start()
     greet(peers + [sibling] + cols)
     far = chips // 2
     plans = [
@@ -289,7 +342,6 @@
         for way in (0, 1):
             step(way, i)
 
-    load.wait()
     gsum[...] = jnp.zeros_like(gsum)
 
     @pl.loop(0, n_row)
@@ -412,10 +464,9 @@
             jax.ShapeDtypeStruct((seg, in_width), bf16),
             jax.ShapeDtypeStruct((in_width, out_width), f32),
         ),
-        in_specs=[VMEM_SPEC, pl.BlockSpec(memory_space=pl.ANY), VMEM_SPEC],
+        in_specs=[VMEM_SPEC] * 3,
         out_specs=(VMEM_SPEC, VMEM_SPEC),
         scratch_shapes=[
-            pltpu.VMEM(feature_panel.shape, bf16),
             pltpu.VMEM((2, count, half, feat_width), bf16),
             pltpu.VMEM((2, half, feat_width), bf16),
             pltpu.VMEM((2, count, half, feat_width), bf16),
@@ -428,7 +479,6 @@
             pltpu.VMEM((n_col - 1, each, out_width), f32),
             pltpu.VMEM((2, each, out_width), f32),
             pltpu.VMEM((2, chips, each, out_width), f32),
-            dma,
             dma((2, count)),
             dma((2, count)),
             dma((2, count)),
@@ -445,65 +495,40 @@
             dma((2,)),
         ],
         compiler_params=pltpu.CompilerParams(
-            collective_id=2, has_side_effects=True, vmem_limit_bytes=LIMIT
+            collective_id=2, has_side_effects=True, vmem_limit_bytes=grant(10 * back_terms.size)
         ),
         name="scatter",
     )(back_terms, feature_panel, weight)
 
 
-def spread_kernel(transpose, read_ids, write_ids, count_ref, tiles_hbm, panel_ref, out_ref, buf, acc, sems):
-    slots, tile_size, _ = tiles_hbm.shape
+def spread_kernel(transpose, plan_ref, tiles_ref, panel_ref, out_ref, acc):
+    tile_size = tiles_ref.shape[1]
     out_tiles = out_ref.shape[0] // tile_size
-    chunks = slots // CHUNK
-    count = count_ref[0]
-    live_chunks = (count + CHUNK - 1) // CHUNK
-
-    def fetch(chunk):
-        part = pl.ds(chunk * CHUNK, CHUNK)
-        return pltpu.make_async_copy(tiles_hbm.at[part], buf.at[part], sems.at[chunk])
-
-    for chunk in range(chunks):
-
-        @pl.when(chunk < live_chunks)
-        def _():
-            fetch(chunk).start()
-
+    pairs = plan_ref[0, plan_ref.shape[1] - 1]
     acc[...] = jnp.zeros_like(acc)
     contract = (((0,), (0,)), ((), ())) if transpose else (((1,), (0,)), ((), ()))
 
-    def one(slot, keep):
-        src = pl.multiple_of(read_ids[slot] * tile_size, tile_size)
-        product = lax.dot_general(
-            buf[slot], panel_ref[pl.ds(src, tile_size), :], contract, preferred_element_type=jnp.float32
-        )
-        return jnp.where(keep, product, 0.0) if keep is not None else product
-
-    def add(slot, product):
-        dst = pl.multiple_of(write_ids[slot] * tile_size, tile_size)
-        acc[pl.ds(dst, tile_size), :] += product
-
-    def chunk_step(chunk, carry):
-        fetch(chunk).wait()
-        base = chunk * CHUNK
-        groups = jnp.minimum(count - base, CHUNK) // GROUP
-
-        def group_step(group, carry):
-            first = base + group * GROUP
-            products = [one(first + k, None) for k in range(GROUP)]
-            for k in range(GROUP):
-                add(first + k, products[k])
-            return carry
-
-        lax.fori_loop(0, groups, group_step, 0)
-
-        def tail_step(slot, carry):
-            add(slot, one(slot, None))
-            return carry
-
-        lax.fori_loop(base + groups * GROUP, jnp.minimum(count, base + CHUNK), tail_step, 0)
+    def read_rows(entry):
+        return panel_ref[pl.ds(pl.multiple_of(plan_ref[1, entry] * tile_size, tile_size), tile_size), :]
+
+    def product(pair):
+        entries = (2 * pair, 2 * pair + 1)
+        left = jnp.concatenate([tiles_ref[plan_ref[0, e]] for e in entries], axis=0 if transpose else 1)
+        right = jnp.concatenate([read_rows(e) for e in entries], axis=0)
+        return lax.dot_general(left, right, contract, preferred_element_type=jnp.float32)
+
+    def add(pair, value):
+        dst = pl.multiple_of(plan_ref[2, 2 * pair] * tile_size, tile_size)
+        acc[pl.ds(dst, tile_size), :] += value
+
+    def group_step(group, carry):
+        first = group * GROUP
+        values = [product(first + k) for k in range(GROUP)]
+        for k in range(GROUP):
+            add(first + k, values[k])
         return carry
 
-    lax.fori_loop(0, live_chunks, chunk_step, 0)
+    lax.fori_loop(0, (pairs + GROUP - 1) // GROUP, group_step, 0)
 
     def finish(tile, carry):
         part = pl.ds(pl.multiple_of(tile * tile_size, tile_size), tile_size)
@@ -513,38 +538,55 @@
     lax.fori_loop(0, out_tiles, finish, 0)
 
 
-def spread_tiles(tiles, read_ids, write_ids, count, panel, out_rows, transpose):
-    slots, tile_size, _ = tiles.shape
+def spread_tiles(tiles, plan, panel, out_rows, transpose):
     feat_width = panel.shape[-1]
     return pl.pallas_call(
         functools.partial(spread_kernel, transpose),
         out_shape=jax.ShapeDtypeStruct((out_rows, feat_width), jnp.bfloat16),
-        in_specs=[
-            pl.BlockSpec(memory_space=pltpu.SMEM),
-            pl.BlockSpec(memory_space=pltpu.SMEM),
-            pl.BlockSpec(memory_space=pltpu.SMEM),
-            pl.BlockSpec(memory_space=pl.ANY),
-            pl.BlockSpec(memory_space=pltpu.VMEM),
-        ],
-        out_specs=pl.BlockSpec(memory_space=pltpu.VMEM),
-        scratch_shapes=[
-            pltpu.VMEM(tiles.shape, tiles.dtype),
-            pltpu.VMEM((out_rows, feat_width), jnp.float32),
-            pltpu.SemaphoreType.DMA((slots // CHUNK,)),
-        ],
-        compiler_params=pltpu.CompilerParams(vmem_limit_bytes=LIMIT),
+        in_specs=[pl.BlockSpec(memory_space=pltpu.SMEM), VMEM_SPEC, VMEM_SPEC],
+        out_specs=VMEM_SPEC,
+        scratch_shapes=[pltpu.VMEM((out_rows, feat_width), jnp.float32)],
+        compiler_params=pltpu.CompilerParams(
+            vmem_limit_bytes=grant(2 * tiles.size + 2 * panel.size + 6 * out_rows * feat_width)
+        ),
         name="back" if transpose else "forth",
-    )(read_ids, write_ids, count, tiles, panel)
+    )(plan, tiles, panel)
+
+
+def finish_kernel(a_ref, b_ref, a_out, b_out, sems):
+    copies = [
+        pltpu.make_async_copy(a_ref, a_out, sems.at[0]),
+        pltpu.make_async_copy(b_ref, b_out, sems.at[1]),
+    ]
+    for copy in copies:
+        copy.start()
+    for copy in copies:
+        copy.wait()
+
+
+def finish(a, b):
+    hbm = pl.BlockSpec(memory_space=pltpu.MemorySpace.HBM)
+    return pl.pallas_call(
+        finish_kernel,
+        out_shape=(jax.ShapeDtypeStruct(a.shape, a.dtype), jax.ShapeDtypeStruct(b.shape, b.dtype)),
+        in_specs=[VMEM_SPEC] * 2,
+        out_specs=(hbm, hbm),
+        scratch_shapes=[pltpu.SemaphoreType.DMA((2,))],
+        compiler_params=pltpu.CompilerParams(vmem_limit_bytes=grant(2 * a.size + 4 * b.size)),
+        name="finish",
+    )(a, b)
 
 
 def body(features, grad_out, weight, tiles, tile_row, tile_col, tile_count):
     segment = features.shape[0]
     n_row, n_col = lax.axis_size("row"), lax.axis_size("col")
-    feature_panel, panel = gather_mixed(features, weight, n_row)
-    partial_value = spread_tiles(tiles, tile_col, tile_row, tile_count, panel, segment * n_col, False)
+    feature_panel, panel, held, forth_plan, back_plan = gather_mixed(
+        features, weight, tiles, tile_row, tile_col, tile_count, n_row
+    )
+    partial_value = spread_tiles(held, forth_plan, panel, segment * n_col, False)
     grad_block = exchange(partial_value, grad_out, n_col)
-    back_terms = spread_tiles(tiles, tile_row, tile_col, tile_count, grad_block, segment * n_row, True)
-    return scatter_sum(back_terms, feature_panel, weight, n_row, n_col)
+    back_terms = spread_tiles(held, back_plan, grad_block, segment * n_row, True)
+    return finish(*scatter_sum(back_terms, feature_panel, weight, n_row, n_col))
 
 
 def solution(mesh):

time: 112 us -> 88.2 us (0.79)
  Pallas kernels: 108 us -> 80.8 us
  local copies, waits for them, and re-layouts: 3.34 us -> 6 us
    pallas_call x1, Pallas kernels: 24.1 us -> 14.3 us  [exchange(): pl.pallas_call(functools.partial(exchange_kernel, n_col), out_shape=jax.S...]
    pallas_call x1, Pallas kernels: 40.4 us -> 32.9 us  [scatter_sum(): pl.pallas_call(functools.partial(scatter_kernel, n_row, n_col), out_shape...]
    pallas_call x2, Pallas kernels: 12.7 us -> 5.68 us  [spread_tiles(): pl.pallas_call(functools.partial(spread_kernel, transpose), out_shape=jax...]
    pallas_call x1, Pallas kernels: 30.8 us -> 27.1 us  [gather_mixed(): pl.pallas_call(functools.partial(gather_kernel, n_row), out_shape=(shape,...]
    unnamed x2 -> x14, local copies, waits for them, and re-layouts: 3.34 us -> 6 us
where the time goes in v3:
time: 88.2 us; the launch traced here: 88.1 us
  Pallas kernels  80.8 us (92%)
  local copies, waits for them, and re-layouts  6 us (7%)
  between operations  1.36 us (2%)
    pallas_call x1, Pallas kernels, scatter_sum(): pl.pallas_call(functools.partial(scatter_kernel, n_row, n_col), out_shape...  32.9 us
    pallas_call x1, Pallas kernels, gather_mixed(): pl.pallas_call(functools.partial(gather_kernel, n_row), out_shape=(shape,...  27.1 us
    pallas_call x1, Pallas kernels, exchange(): pl.pallas_call(functools.partial(exchange_kernel, n_col), out_shape=jax.S...  14.3 us
    unnamed x14, local copies, waits for them, and re-layouts  6 us
    pallas_call x2, Pallas kernels, spread_tiles(): pl.pallas_call(functools.partial(spread_kernel, transpose), out_shape=jax...  5.68 us

profile of v3, /device:TPU:0, one launch (start us, length us, event | category | flops | bytes accessed | tf_op | source)
XLA Modules:
  0.0 88.1 jit_solution(10270052808655392452)
XLA Ops:
  1.3 0.0 copy-start
  1.3 2.8 %copy-done = bf16[192,128,128]{2,1,0:T(8,128)(2,1)S(1)} copy-done((bf16[192,128,128]{2,1,0:T(8,128)(2,1)S(1)}, bf16[192,128,128]{2,1,0:T(8,128)(2,1)}, u32[]{:S(2)}) %copy-start) | copy-done | bytes 6291480
  4.1 0.0 copy-start.1
  4.1 0.9 %copy-done.1 = bf16[256,256]{1,0:T(8,128)(2,1)S(1)} copy-done((bf16[256,256]{1,0:T(8,128)(2,1)S(1)}, bf16[256,256]{1,0:T(8,128)(2,1)}, u32[]{:S(2)}) %copy-start.1) | copy-done | bytes 131096
  5.0 0.0 copy-start.3
  5.0 0.9 %copy-done.3 = bf16[512,256]{1,0:T(8,128)(2,1)S(1)} copy-done((bf16[512,256]{1,0:T(8,128)(2,1)S(1)}, bf16[512,256]{1,0:T(8,128)(2,1)}, u32[]{:S(2)}) %copy-start.3) | copy-done | bytes 262168
  5.9 0.0 copy-start.5
  5.9 0.7 copy-done.5
  6.6 0.0 copy-start.6
  6.6 0.7 copy-done.6
  7.3 27.1 %gather.1 = (bf16[8192,256]{1,0:T(8,128)(2,1)S(1)}, bf16[8192,256]{1,0:T(8,128)(2,1)S(1)}, bf16[193,128,128]{2,1,0:T(8,128)(2,1)S(1)}, s32[3,384]{1,0:T(4,128)S(1)}, s32[3,384]{1,0:T(4,128)S(1)}) custom-call(s32[1]{0:T(128)S(6)} %copy.9.count_ref, bf16[512,256]{1,0:T(8,128)(2,1)S(1)} %copy-done.3, bf16[256,256]{1,0:T(8,128)(2,1)S(1)} %copy-done.1, ...), custom_call_target="tpu_custom_call" | custom-call | tf_op jit(solution)/shard_map/gather/pallas_call | solution.py:196
  34.4 0.0 copy-start.4
  34.4 2.1 %forth.1.part_ref = bf16[1024,256]{1,0:T(8,128)(2,1)S(1)} custom-call(s32[3,384]{1,0:T(4,128)S(1)} %get-tuple-element.11.plan_ref, bf16[193,128,128]{2,1,0:T(8,128)(2,1)S(1)} %get-tuple-element.10.tiles_ref, bf16[8192,256]{1,0:T(8,128)(2,1)S(1)} %get-tuple-element.12.panel_ref), custom_call_target="tpu_custom_call" | custom-call | tf_op jit(solution)/shard_map/forth/pallas_call | solution.py:543
  36.5 0.0 copy-done.4
  36.5 14.3 %exchange.1.panel_ref = bf16[1024,256]{1,0:T(8,128)(2,1)S(1)} custom-call(bf16[1024,256]{1,0:T(8,128)(2,1)S(1)} %forth.1.part_ref, bf16[512,256]{1,0:T(8,128)(2,1)S(1)} %copy-done.4), custom_call_target="tpu_custom_call" | custom-call | tf_op jit(solution)/shard_map/exchange/pallas_call | solution.py:263
  50.8 0.0 copy-start.2
  50.8 3.6 %back.1.back_ref = bf16[8192,256]{1,0:T(8,128)(2,1)S(1)} custom-call(s32[3,384]{1,0:T(4,128)S(1)} %get-tuple-element.9.plan_ref, bf16[193,128,128]{2,1,0:T(8,128)(2,1)S(1)} %get-tuple-element.10.tiles_ref, bf16[1024,256]{1,0:T(8,128)(2,1)S(1)} %exchange.1.panel_ref), custom_call_target="tpu_custom_call" | custom-call | tf_op jit(solution)/shard_map/back/pallas_call | solution.py:543
  54.4 0.0 copy-done.2
  54.5 32.9 %scatter.1 = (bf16[512,256]{1,0:T(8,128)(2,1)S(1)}, f32[256,256]{1,0:T(8,128)S(1)}) custom-call(bf16[8192,256]{1,0:T(8,128)(2,1)S(1)} %back.1.back_ref, bf16[8192,256]{1,0:T(8,128)(2,1)S(1)} %get-tuple-element.13.fp_ref, bf16[256,256]{1,0:T(8,128)(2,1)S(1)} %copy-done.2), custom_call_target="tpu_custom_call" | custom-call | tf_op jit(solution)/shard_map/scatter/pallas_call | solution.py:461
  87.3 0.8 finish.1
Async XLA Ops:
  1.3 2.8 %copy-start = (bf16[192,128,128]{2,1,0:T(8,128)(2,1)S(1)}, bf16[192,128,128]{2,1,0:T(8,128)(2,1)}, u32[]{:S(2)}) copy-start(bf16[192,128,128]{2,1,0:T(8,128)(2,1)} %tiles_hbm.1) | copy-start | bytes 18874372
  4.1 0.9 %copy-start.1 = (bf16[256,256]{1,0:T(8,128)(2,1)S(1)}, bf16[256,256]{1,0:T(8,128)(2,1)}, u32[]{:S(2)}) copy-start(bf16[256,256]{1,0:T(8,128)(2,1)} %w_ref.3) | copy-start | bytes 393220
  5.0 0.9 %copy-start.3 = (bf16[512,256]{1,0:T(8,128)(2,1)S(1)}, bf16[512,256]{1,0:T(8,128)(2,1)}, u32[]{:S(2)}) copy-start(bf16[512,256]{1,0:T(8,128)(2,1)} %f_ref.1) | copy-start | bytes 786436
  5.9 0.7 copy-start.5
  6.6 0.7 copy-start.6
  34.4 2.1 %copy-start.4 = (bf16[512,256]{1,0:T(8,128)(2,1)S(1)}, bf16[512,256]{1,0:T(8,128)(2,1)}, u32[]{:S(2)}) copy-start(bf16[512,256]{1,0:T(8,128)(2,1)} %up_ref.1) | copy-start | bytes 786436
  50.8 3.6 %copy-start.2 = (bf16[256,256]{1,0:T(8,128)(2,1)S(1)}, bf16[256,256]{1,0:T(8,128)(2,1)}, u32[]{:S(2)}) copy-start(bf16[256,256]{1,0:T(8,128)(2,1)} %w_ref.3) | copy-start | bytes 393220

commit v4 on v3

--- a/solution.py
+++ b/solution.py
@@ -85,10 +85,18 @@
 
 
 def gather_kernel(
-    n_row, count_ref, f_ref, w_ref, tr_ref, tc_ref, tiles_hbm,
+    n_row, count_ref, f_hbm, w_hbm, tr_hbm, tc_hbm, tiles_hbm,
     fp_ref, mp_ref, tiles_ref, forth_ref, back_ref,
-    ssem, rsem, xs, xr, os, orr, tsem,
+    f_ref, w_ref, tr_ref, tc_ref, ssem, rsem, xs, xr, os, orr, tsem, isem,
 ):
+    inputs = [
+        pltpu.make_async_copy(src, dst, isem.at[at])
+        for at, (src, dst) in enumerate(
+            ((f_hbm, f_ref), (w_hbm, w_ref), (tr_hbm, tr_ref), (tc_hbm, tc_ref))
+        )
+    ]
+    for copy in inputs:
+        copy.start()
     slots = tiles_hbm.shape[0]
     load = pltpu.make_async_copy(tiles_hbm, tiles_ref.at[pl.ds(0, slots)], tsem)
     load.start()
@@ -103,6 +111,7 @@
     nexts = [row_device(ring_chip(place + way, chips), core) for way in ways]
     sibling = row_device(chip, 1 - core)
     greet(nexts + [sibling])
+    inputs[0].wait()
     far = chips // 2
     plans = [
         [(h, k) for k in range(1, far) for h in (way, 1 - way)] + [(way, far)] for way in (0, 1)
@@ -146,6 +155,8 @@
             hop(way, i).start()
     for h in (0, 1):
         own_across(h).start()
+    for copy in inputs[1:]:
+        copy.wait()
     fp_ref[pl.ds(pl.multiple_of(me * seg, seg), seg), :] = f_ref[...]
     for h in (0, 1):
         mix(me, h)
@@ -197,17 +208,32 @@
         functools.partial(gather_kernel, n_row),
         out_shape=(shape, shape, held, plan, plan),
         in_specs=[pl.BlockSpec(memory_space=pltpu.SMEM)]
-        + [VMEM_SPEC] * 4
-        + [pl.BlockSpec(memory_space=pltpu.MemorySpace.HBM)],
+        + [pl.BlockSpec(memory_space=pltpu.MemorySpace.HBM)] * 5,
         out_specs=(VMEM_SPEC,) * 5,
-        scratch_shapes=[dma((2, count))] * 4 + [dma((2,))] * 2 + [dma],
+        scratch_shapes=[
+            pltpu.VMEM(features.shape, features.dtype),
+            pltpu.VMEM(weight.shape, weight.dtype),
+            pltpu.VMEM((1, slots), jnp.int32),
+            pltpu.VMEM((1, slots), jnp.int32),
+        ]
+        + [dma((2, count))] * 4
+        + [dma((2,))] * 2
+        + [dma, dma((4,))],
         compiler_params=pltpu.CompilerParams(
             collective_id=0,
             has_side_effects=True,
             vmem_limit_bytes=grant(4 * shape.size + 2 * held.size + 2 * features.size),
         ),
         name="gather",
-    )(tile_count, features, weight, tile_row.reshape(1, slots), tile_col.reshape(1, slots), tiles)
+    )(
+        tile_count,
+        *(
+            pltpu.with_memory_space_constraint(array, pltpu.MemorySpace.HBM)
+            for array in (
+                features, weight, tile_row.reshape(1, slots), tile_col.reshape(1, slots), tiles
+            )
+        ),
+    )
 
 
 PARTS = 4

time: 88.2 us -> 82.1 us (0.931); the launches traced: 88.1 us -> 83.2 us
  local copies, waits for them, and re-layouts: 6 us -> 0.01 us
  Pallas kernels: 80.8 us -> 81.8 us
    unnamed x14 -> x4, local copies, waits for them, and re-layouts: 6 us -> 0.01 us
    pallas_call x1, Pallas kernels: 32.9 us -> 35.4 us  [scatter_sum(): pl.pallas_call(functools.partial(scatter_kernel, n_row, n_col), out_shape...]
where the time goes in v4:
time: 82.1 us; the launch traced here: 83.2 us
  Pallas kernels  81.8 us (100%)
  between operations  1.35 us (2%)
    pallas_call x1, Pallas kernels, scatter_sum(): pl.pallas_call(functools.partial(scatter_kernel, n_row, n_col), out_shape...  35.4 us
    pallas_call x1, Pallas kernels, gather_mixed(): pl.pallas_call(functools.partial(gather_kernel, n_row), out_shape=(shape,...  26.7 us
    pallas_call x1, Pallas kernels, exchange(): pl.pallas_call(functools.partial(exchange_kernel, n_col), out_shape=jax.S...  13.8 us
    pallas_call x2, Pallas kernels, spread_tiles(): pl.pallas_call(functools.partial(spread_kernel, transpose), out_shape=jax...  4.97 us

profile of v4, /device:TPU:0, one launch (start us, length us, event | category | flops | bytes accessed | tf_op | source)
XLA Modules:
  0.0 83.2 jit_solution(8953636803360359928)
XLA Ops:
  1.3 26.7 %gather.1 = (bf16[8192,256]{1,0:T(8,128)(2,1)S(1)}, bf16[8192,256]{1,0:T(8,128)(2,1)S(1)}, bf16[193,128,128]{2,1,0:T(8,128)(2,1)S(1)}, s32[3,384]{1,0:T(4,128)S(1)}, s32[3,384]{1,0:T(4,128)S(1)}) custom-call(s32[1]{0:T(128)S(6)} %copy.9.count_ref, bf16[512,256]{1,0:T(8,128)(2,1)} %f_hbm.1, bf16[256,256]{1,0:T(8,128)(2,1)} %w_ref.1, s32[1,192]{1,0:T(1,128)} %bitcast.2, ...), custom_call_target="tpu_custom_call" | custom-call | tf_op jit(solution)/shard_map/gather/pallas_call | solution.py:207
  28.0 0.0 copy-start.1
  28.0 1.8 %forth.1.part_ref = bf16[1024,256]{1,0:T(8,128)(2,1)S(1)} custom-call(s32[3,384]{1,0:T(4,128)S(1)} %get-tuple-element.11.plan_ref, bf16[193,128,128]{2,1,0:T(8,128)(2,1)S(1)} %get-tuple-element.10.tiles_ref, bf16[8192,256]{1,0:T(8,128)(2,1)S(1)} %get-tuple-element.12.panel_ref), custom_call_target="tpu_custom_call" | custom-call | tf_op jit(solution)/shard_map/forth/pallas_call | solution.py:569
  29.8 0.0 copy-done.1
  29.8 13.8 %exchange.1.panel_ref = bf16[1024,256]{1,0:T(8,128)(2,1)S(1)} custom-call(bf16[1024,256]{1,0:T(8,128)(2,1)S(1)} %forth.1.part_ref, bf16[512,256]{1,0:T(8,128)(2,1)S(1)} %copy-done.1), custom_call_target="tpu_custom_call" | custom-call | tf_op jit(solution)/shard_map/exchange/pallas_call | solution.py:289
  43.6 0.0 copy-start
  43.7 3.2 %back.1.back_ref = bf16[8192,256]{1,0:T(8,128)(2,1)S(1)} custom-call(s32[3,384]{1,0:T(4,128)S(1)} %get-tuple-element.9.plan_ref, bf16[193,128,128]{2,1,0:T(8,128)(2,1)S(1)} %get-tuple-element.10.tiles_ref, bf16[1024,256]{1,0:T(8,128)(2,1)S(1)} %exchange.1.panel_ref), custom_call_target="tpu_custom_call" | custom-call | tf_op jit(solution)/shard_map/back/pallas_call | solution.py:569
  46.9 0.0 copy-done
  46.9 35.4 %scatter.1 = (bf16[512,256]{1,0:T(8,128)(2,1)S(1)}, f32[256,256]{1,0:T(8,128)S(1)}) custom-call(bf16[8192,256]{1,0:T(8,128)(2,1)S(1)} %back.1.back_ref, bf16[8192,256]{1,0:T(8,128)(2,1)S(1)} %get-tuple-element.13.fp_ref, bf16[256,256]{1,0:T(8,128)(2,1)S(1)} %copy-done), custom_call_target="tpu_custom_call" | custom-call | tf_op jit(solution)/shard_map/scatter/pallas_call | solution.py:487
  82.3 0.8 finish.1
Async XLA Ops:
  28.0 1.8 %copy-start.1 = (bf16[512,256]{1,0:T(8,128)(2,1)S(1)}, bf16[512,256]{1,0:T(8,128)(2,1)}, u32[]{:S(2)}) copy-start(bf16[512,256]{1,0:T(8,128)(2,1)} %up_ref.1) | copy-start | bytes 786436
  43.6 3.2 %copy-start = (bf16[256,256]{1,0:T(8,128)(2,1)S(1)}, bf16[256,256]{1,0:T(8,128)(2,1)}, u32[]{:S(2)}) copy-start(bf16[256,256]{1,0:T(8,128)(2,1)} %w_ref.1) | copy-start | bytes 393220

commit v5 on v4

--- a/solution.py
+++ b/solution.py
@@ -236,7 +236,7 @@
     )
 
 
-PARTS = 4
+PARTS = 8
 
 
 def exchange_kernel(n_col, part_ref, up_ref, out_ref, inbox, ssem, rsem, gs, gr):
@@ -370,21 +370,26 @@
 
     gsum[...] = jnp.zeros_like(gsum)
 
-    @pl.loop(0, n_row)
-    def _(block):
-        rows = pl.ds(pl.multiple_of(block * seg, seg), seg)
-        gsum[...] += lax.dot_general(
-            fp_ref[rows, :], back_ref[rows, :], (((0,), (0,)), ((), ())), preferred_element_type=jnp.float32
-        )
-
+    def terms(first, past):
+        @pl.loop(first, past)
+        def _(block):
+            rows = pl.ds(pl.multiple_of(block * seg, seg), seg)
+            gsum[...] += lax.dot_general(
+                fp_ref[rows, :], back_ref[rows, :], (((0,), (0,)), ((), ())), preferred_element_type=jnp.float32
+            )
+
+    terms(0, chips)
     own_rows = gw_ref.shape[0] // 2
 
     def half_rows(which):
         return pl.ds(pl.multiple_of(which * own_rows, own_rows), own_rows)
 
-    gsib_out[...] = gsum[half_rows(1 - core), :].astype(gsib_out.dtype)
     sib_copy = remote(gsib_out, gsib_in, ga.at[0], ga.at[1], sibling)
-    sib_copy.start()
+
+    def stage_a():
+        terms(chips, n_row)
+        gsib_out[...] = gsum[half_rows(1 - core), :].astype(gsib_out.dtype)
+        sib_copy.start()
 
     def spread(o):
         return remote(
@@ -437,7 +442,7 @@
             collect(o).wait_recv()
         last_copy.start()
 
-    stages = {2: stage_b, 4: stage_c, 5: stage_d}
+    stages = {2: stage_a, 3: stage_b, 4: stage_c, 5: stage_d}
     for i in range(2, count):
         for way in (0, 1):
             step(way, i)

time: 82.1 us -> 82.8 us (level); the launches traced: 83.2 us -> 82.3 us
  Pallas kernels: 81.8 us -> 80.9 us
    pallas_call x1, Pallas kernels: 13.8 us -> 13 us  [exchange(): pl.pallas_call(functools.partial(exchange_kernel, n_col), out_shape=jax.S...]
where the time goes in v5:
time: 82.8 us; the launch traced here: 82.3 us
  Pallas kernels  80.9 us (98%)
  between operations  1.35 us (2%)
    pallas_call x1, Pallas kernels, scatter_sum(): pl.pallas_call(functools.partial(scatter_kernel, n_row, n_col), out_shape...  35.8 us
    pallas_call x1, Pallas kernels, gather_mixed(): pl.pallas_call(functools.partial(gather_kernel, n_row), out_shape=(shape,...  26.7 us
    pallas_call x1, Pallas kernels, exchange(): pl.pallas_call(functools.partial(exchange_kernel, n_col), out_shape=jax.S...  13 us
    pallas_call x2, Pallas kernels, spread_tiles(): pl.pallas_call(functools.partial(spread_kernel, transpose), out_shape=jax...  4.65 us

profile of v5, /device:TPU:0, one launch (start us, length us, event | category | flops | bytes accessed | tf_op | source)
XLA Modules:
  0.0 82.3 jit_solution(6756405142230986777)
XLA Ops:
  1.3 26.7 %gather.1 = (bf16[8192,256]{1,0:T(8,128)(2,1)S(1)}, bf16[8192,256]{1,0:T(8,128)(2,1)S(1)}, bf16[193,128,128]{2,1,0:T(8,128)(2,1)S(1)}, s32[3,384]{1,0:T(4,128)S(1)}, s32[3,384]{1,0:T(4,128)S(1)}) custom-call(s32[1]{0:T(128)S(6)} %copy.9.count_ref, bf16[512,256]{1,0:T(8,128)(2,1)} %f_hbm.1, bf16[256,256]{1,0:T(8,128)(2,1)} %w_ref.1, s32[1,192]{1,0:T(1,128)} %bitcast.2, ...), custom_call_target="tpu_custom_call" | custom-call | tf_op jit(solution)/shard_map/gather/pallas_call | solution.py:207
  28.0 0.0 copy-start.1
  28.0 1.4 %forth.1.part_ref = bf16[1024,256]{1,0:T(8,128)(2,1)S(1)} custom-call(s32[3,384]{1,0:T(4,128)S(1)} %get-tuple-element.11.plan_ref, bf16[193,128,128]{2,1,0:T(8,128)(2,1)S(1)} %get-tuple-element.10.tiles_ref, bf16[8192,256]{1,0:T(8,128)(2,1)S(1)} %get-tuple-element.12.panel_ref), custom_call_target="tpu_custom_call" | custom-call | tf_op jit(solution)/shard_map/forth/pallas_call | solution.py:574
  29.5 0.0 copy-done.1
  29.5 13.0 %exchange.1.panel_ref = bf16[1024,256]{1,0:T(8,128)(2,1)S(1)} custom-call(bf16[1024,256]{1,0:T(8,128)(2,1)S(1)} %forth.1.part_ref, bf16[512,256]{1,0:T(8,128)(2,1)S(1)} %copy-done.1), custom_call_target="tpu_custom_call" | custom-call | tf_op jit(solution)/shard_map/exchange/pallas_call | solution.py:289
  42.5 0.0 copy-start
  42.5 3.2 %back.1.back_ref = bf16[8192,256]{1,0:T(8,128)(2,1)S(1)} custom-call(s32[3,384]{1,0:T(4,128)S(1)} %get-tuple-element.9.plan_ref, bf16[193,128,128]{2,1,0:T(8,128)(2,1)S(1)} %get-tuple-element.10.tiles_ref, bf16[1024,256]{1,0:T(8,128)(2,1)S(1)} %exchange.1.panel_ref), custom_call_target="tpu_custom_call" | custom-call | tf_op jit(solution)/shard_map/back/pallas_call | solution.py:574
  45.7 0.0 copy-done
  45.7 35.8 %scatter.1 = (bf16[512,256]{1,0:T(8,128)(2,1)S(1)}, f32[256,256]{1,0:T(8,128)S(1)}) custom-call(bf16[8192,256]{1,0:T(8,128)(2,1)S(1)} %back.1.back_ref, bf16[8192,256]{1,0:T(8,128)(2,1)S(1)} %get-tuple-element.13.fp_ref, bf16[256,256]{1,0:T(8,128)(2,1)S(1)} %copy-done), custom_call_target="tpu_custom_call" | custom-call | tf_op jit(solution)/shard_map/scatter/pallas_call | solution.py:492
  81.5 0.8 finish.1
Async XLA Ops:
  28.0 1.5 %copy-start.1 = (bf16[512,256]{1,0:T(8,128)(2,1)S(1)}, bf16[512,256]{1,0:T(8,128)(2,1)}, u32[]{:S(2)}) copy-start(bf16[512,256]{1,0:T(8,128)(2,1)} %up_ref.1) | copy-start | bytes 786436
  42.5 3.2 %copy-start = (bf16[256,256]{1,0:T(8,128)(2,1)S(1)}, bf16[256,256]{1,0:T(8,128)(2,1)}, u32[]{:S(2)}) copy-start(bf16[256,256]{1,0:T(8,128)(2,1)} %w_ref.1) | copy-start | bytes 393220
